TPU v7x, 512 devices: a whole 4x8x8 slice. The times are simulated.
512 devices in a mesh: shot: 16 (over y_hi, x, core), gx: 4 (over y_lo), gy: 8 (over z).
Axes of the slice: x: 4, y: 8 (y_hi: 2, y_lo: 4; y = y_hi * 4 + y_lo), z: 8, core: 2. Of those that a mesh axis runs over, the one named last changes fastest.
Arguments:
- forward_state: bfloat16 [16, 9, 16, 32, 1024], P('shot', None, None, 'gx', 'gy'), may hold values from -6 to 6
- adjoint_state: bfloat16 [16, 9, 16, 32, 1024], P('shot', None, None, 'gx', 'gy'), may hold values from -6 to 6
- lame: float32 [16, 32, 1024], P(None, 'gx', 'gy'), may hold values from 1 to 3
- shear: float32 [16, 32, 1024], P(None, 'gx', 'gy'), may hold values from 0.5 to 1.5
- density: float32 [16, 32, 1024], P(None, 'gx', 'gy'), may hold values from 1 to 2
- wavelet: float32 [16, 3], P('shot'), may hold values from -60 to 60
- residual: float32 [16, 3, 256], P('shot'), may hold values from -60 to 60
- source_x: int32 [16], P('shot'), may hold values from 0 to 31
- source_y: int32 [16], P('shot'), may hold values from 0 to 1023
- receiver_x: int32 [16, 256], P('shot'), may hold values from 0 to 31
- receiver_y: int32 [16, 256], P('shot'), may hold values from 0 to 1023
- aperture: int32 [16, 4, 8], P('shot', 'gx', 'gy'), may hold values 0 or 1
Outputs:
- grad_lambda: float32 [16, 32, 1024], P('shot', 'gx', 'gy')
- grad_mu: float32 [16, 32, 1024], P('shot', 'gx', 'gy')
- grad_rho: float32 [16, 32, 1024], P('shot', 'gx', 'gy')
All inputs are finite; a program needn't handle non-finite values. No bound on the sum of `aperture` on one device may be relied on, other than what follows from the above.
Results may differ from a plain program's by a relative error of at most 0.0005.
Values may be sent and summed in bfloat16 or wider, within the bound.
A program may use at most 64 MiB of HBM per device.

v0:
```python
import jax
import jax.numpy as jnp
from jax import lax
from jax.sharding import PartitionSpec as P

courant = 0.2


def from_behind(value, axis, steps):
    count = lax.axis_size(axis)
    first, last = (max(0, -steps), min(count, count - steps))
    return lax.ppermute(value, axis, [(source, source + steps) for source in range(first, last)])


def above_x(stack):
    return from_behind(stack[:, :, 0:1, :], "gx", -1)


def below_x(stack):
    return from_behind(stack[:, :, -1:, :], "gx", 1)


def above_y(stack):
    return from_behind(stack[:, :, :, 0:1], "gy", -1)


def below_y(stack):
    return from_behind(stack[:, :, :, -1:], "gy", 1)


def ahead(field, edge, axis):
    size = field.shape[axis]
    tail = lax.slice_in_dim(field, 1, size, axis=axis)
    return jnp.concatenate([tail, edge], axis=axis) - field


def behind(field, edge, axis):
    size = field.shape[axis]
    head = lax.slice_in_dim(field, 0, size - 1, axis=axis)
    return field - jnp.concatenate([edge, head], axis=axis)


def depth_ahead(field):
    return ahead(field, jnp.zeros_like(field[:1]), 0)


def depth_behind(field):
    return behind(field, jnp.zeros_like(field[:1]), 0)


def velocity_update(velocity, stress, buoyancy):
    upper_x = above_x(stress[0][None])
    lower_x = below_x(jnp.stack([stress[3], stress[4]]))
    upper_y = above_y(stress[1][None])
    lower_y = below_y(jnp.stack([stress[3], stress[5]]))
    factor = courant * buoyancy
    return (
        velocity[0]
        + factor
        * (
            ahead(stress[0], upper_x[0], 1)
            + behind(stress[3], lower_y[0], 2)
            + depth_behind(stress[4])
        ),
        velocity[1]
        + factor
        * (
            behind(stress[3], lower_x[0], 1)
            + ahead(stress[1], upper_y[0], 2)
            + depth_behind(stress[5])
        ),
        velocity[2]
        + factor
        * (
            behind(stress[4], lower_x[1], 1)
            + behind(stress[5], lower_y[1], 2)
            + depth_ahead(stress[2])
        ),
    )


def strain_parts(velocity):
    upper_x = above_x(jnp.stack([velocity[1], velocity[2]]))
    lower_x = below_x(velocity[0][None])
    upper_y = above_y(jnp.stack([velocity[0], velocity[2]]))
    lower_y = below_y(velocity[1][None])
    return (
        behind(velocity[0], lower_x[0], 1),
        behind(velocity[1], lower_y[0], 2),
        depth_behind(velocity[2]),
        ahead(velocity[0], upper_y[0], 2) + ahead(velocity[1], upper_x[0], 1),
        depth_ahead(velocity[0]) + ahead(velocity[2], upper_x[1], 1),
        depth_ahead(velocity[1]) + ahead(velocity[2], upper_y[1], 2),
    )


def stress_update(stress, strain, lame, shear):
    dilation = strain[0] + strain[1] + strain[2]
    bulk = lame * dilation
    return (
        stress[0] + courant * (bulk + 2.0 * shear * strain[0]),
        stress[1] + courant * (bulk + 2.0 * shear * strain[1]),
        stress[2] + courant * (bulk + 2.0 * shear * strain[2]),
        stress[3] + courant * shear * strain[3],
        stress[4] + courant * shear * strain[4],
        stress[5] + courant * shear * strain[5],
    )


def image_terms(strain, acceleration, adjoint_strain, adjoint_velocity):
    first = (strain[0] + strain[1] + strain[2]) * (
        adjoint_strain[0] + adjoint_strain[1] + adjoint_strain[2]
    )
    second = 2.0 * (
        strain[0] * adjoint_strain[0]
        + strain[1] * adjoint_strain[1]
        + strain[2] * adjoint_strain[2]
    )
    second = (
        second
        + strain[3] * adjoint_strain[3]
        + strain[4] * adjoint_strain[4]
        + strain[5] * adjoint_strain[5]
    )
    third = (
        acceleration[0] * adjoint_velocity[0]
        + acceleration[1] * adjoint_velocity[1]
        + acceleration[2] * adjoint_velocity[2]
    )
    return (first, second, third)


def inject(field, depth, cell_x, cell_y, values, x_start, y_start):
    local_x = cell_x - x_start
    local_y = cell_y - y_start
    inside = (
        (local_x >= 0) & (local_x < field.shape[1]) & (local_y >= 0) & (local_y < field.shape[2])
    )
    local_x = jnp.where(inside, local_x, field.shape[1])
    local_y = jnp.where(inside, local_y, field.shape[2])
    return field.at[depth, local_x, local_y].add(values, mode="drop")


def local(
    forward_state,
    adjoint_state,
    lame,
    shear,
    density,
    wavelet,
    residual,
    source_x,
    source_y,
    receiver_x,
    receiver_y,
    aperture,
):
    tile_x = lame.shape[1]
    tile_y = lame.shape[2]
    x_start = lax.axis_index("gx") * tile_x
    y_start = lax.axis_index("gy") * tile_y
    groups = lax.axis_size("shot")
    steps = wavelet.shape[1]
    buoyancy = 1.0 / density
    factor = -courant / groups * aperture.reshape(()).astype(jnp.float32)
    forward_fields = forward_state[0].astype(jnp.float32)
    adjoint_fields = adjoint_state[0].astype(jnp.float32)
    lame_used, shear_used, buoy_used = (lame, shear, buoyancy)
    velocity = (forward_fields[0], forward_fields[1], forward_fields[2])
    stress = tuple((forward_fields[index] for index in range(3, 9)))
    saved = []
    for step in range(steps):
        new_velocity = velocity_update(velocity, stress, buoy_used)
        strain = strain_parts(new_velocity)
        stress = stress_update(stress, strain, lame_used, shear_used)
        pulse = wavelet[0, step : step + 1]
        stress = (
            tuple(
                (
                    inject(stress[index], 2, source_x, source_y, pulse, x_start, y_start)
                    for index in range(3)
                )
            )
            + stress[3:]
        )
        acceleration = tuple(
            ((new_velocity[index] - velocity[index]) / courant for index in range(3))
        )
        saved.append((strain, acceleration))
        velocity = new_velocity
    adjoint_velocity = (adjoint_fields[0], adjoint_fields[1], adjoint_fields[2])
    adjoint_stress = tuple((adjoint_fields[index] for index in range(3, 9)))
    local_total = jnp.zeros((3,) + lame.shape, jnp.float32)
    for step in range(steps):
        new_velocity = velocity_update(adjoint_velocity, adjoint_stress, buoy_used)
        traces = residual[0, steps - 1 - step]
        lifted = inject(new_velocity[2], 1, receiver_x[0], receiver_y[0], traces, x_start, y_start)
        new_velocity = (new_velocity[0], new_velocity[1], lifted)
        adjoint_strain = strain_parts(new_velocity)
        adjoint_stress = stress_update(adjoint_stress, adjoint_strain, lame_used, shear_used)
        strain, acceleration = saved[steps - 1 - step]
        term = jnp.stack(image_terms(strain, acceleration, adjoint_strain, new_velocity)) * factor
        local_total = local_total + term
        adjoint_velocity = new_velocity
    owned = lax.psum_scatter(local_total, "shot", scatter_dimension=1, tiled=True)
    return (owned[0], owned[1], owned[2])


def solution(mesh):
    return jax.shard_map(
        local,
        mesh=mesh,
        in_specs=(
            P("shot", None, None, "gx", "gy"),
            P("shot", None, None, "gx", "gy"),
            P(None, "gx", "gy"),
            P(None, "gx", "gy"),
            P(None, "gx", "gy"),
            P("shot", None),
            P("shot", None, None),
            P("shot"),
            P("shot"),
            P("shot", None),
            P("shot", None),
            P("shot", "gx", "gy"),
        ),
        out_specs=(P("shot", "gx", "gy"), P("shot", "gx", "gy"), P("shot", "gx", "gy")),
        check_vma=False,
    )
```

profile of v0, /device:TPU:7, one launch (start us, length us, event | category | flops | bytes accessed | tf_op | source)
XLA Modules:
  0.0 496.8 jit_solution(3707130627441366449)
XLA Ops:
  9.1 4.6 collective-permute-start.23
  14.6 4.0 collective-permute-start.1
  18.6 3.2 collective-permute-start.25
  22.5 1.3 collective-permute-start
  24.4 1.3 collective-permute-start.4
  34.6 1.3 collective-permute-start.26
  36.1 1.3 collective-permute-start.22
  38.3 5.2 %collective-permute-start.3 = (f32[2,16,1,128]{3,1,2,0:T(8,128)S(1)}, f32[2,16,1,128]{3,1,2,0:T(8,128)}, u32[]{:S(2)}, u32[]{:S(2)}) collective-permute-start(f32[2,16,1,128]{3,1,2,0:T(8,128)S(1)} %bitcast.515), channel_id=1, source_target_pairs={{0,8},{8,16},{16,24},{1,9},{9,17},{17,25},{2,10},{10,18},{18,26},{... | collective-permute-start | bytes 49160 | tf_op jit(solution)/shard_map/ppermute | solution.py:12
  47.0 15.1 %scatter_fusion = f32[16,8,128]{2,1,0:T(8,128)S(1)} fusion(f32[16,8,128]{2,1,0:T(8,128)S(1)} %copy.601, s32[256]{0:T(256)S(1)} %bitcast.386, f32[256]{0:T(256)S(1)} %bitcast.530), kind=kCustom, calls=%fused_computation | custom fusion | flops 256 | bytes 6144 | tf_op jit(solution)/shard_map/scatter-add | solution.py:141
  62.1 1.3 collective-permute-start.30
  65.3 1.3 collective-permute-start.31
  66.6 4.0 collective-permute-start.24
  70.6 5.3 %collective-permute-start.27 = (f32[1,16,8,1]{3,1,2,0:T(8,128)S(1)}, f32[1,16,8,1]{3,1,2,0:T(8,128)S(1)}, u32[]{:S(2)}, u32[]{:S(2)}) collective-permute-start(f32[1,16,8,1]{3,1,2,0:T(8,128)S(1)} %slice.1236), channel_id=1, source_target_pairs={{0,1},{1,2},{2,3},{3,4},{4,5},{5,6},{6,7},{8,9},{9,10},{10,11},{11... | collective-permute-start | bytes 1544 | tf_op jit(solution)/shard_map/ppermute | solution.py:12
  78.9 2.8 collective-permute-start.35
  82.5 5.2 %collective-permute-start.33 = (f32[2,16,8,1]{3,1,2,0:T(8,128)S(1)}, f32[2,16,8,1]{3,1,2,0:T(8,128)S(1)}, u32[]{:S(2)}, u32[]{:S(2)}) collective-permute-start(f32[2,16,8,1]{3,1,2,0:T(8,128)S(1)} %pad_maximum_fusion.3), channel_id=1, source_target_pairs={{0,1},{1,2},{2,3},{3,4},{4,5},{5,6},{6,7},{8,9},{9,10},{10,11},{11... | collective-permute-start | bytes 3080 | tf_op jit(solution)/shard_map/ppermute | solution.py:12
  87.9 1.3 collective-permute-start.36
  89.2 1.3 collective-permute-start.32
  90.8 2.4 collective-permute-done.36
  94.9 15.1 %scatter_fusion.1 = f32[16,8,128]{2,1,0:T(8,128)S(1)} fusion(f32[16,8,128]{2,1,0:T(8,128)S(1)} %get-tuple-element.190, s32[256]{0:T(256)S(1)} %bitcast.387, f32[256]{0:T(256)S(1)} %bitcast.529), kind=kCustom, calls=%fused_computation.1 | custom fusion | flops 256 | bytes 6144 | tf_op jit(solution)/shard_map/scatter-add | solution.py:141
  110.8 1.3 collective-permute-start.38
  112.2 5.2 %collective-permute-start.37 = (f32[1,16,8,1]{3,2,1,0:T(8,128)S(1)}, f32[1,16,8,1]{3,2,1,0:T(8,128)S(1)}, u32[]{:S(2)}, u32[]{:S(2)}) collective-permute-start(f32[1,16,8,1]{3,2,1,0:T(8,128)S(1)} %slice.1278), channel_id=1, source_target_pairs={{0,1},{1,2},{2,3},{3,4},{4,5},{5,6},{6,7},{8,9},{9,10},{10,11},{11... | collective-permute-start | bytes 1544 | tf_op jit(solution)/shard_map/ppermute | solution.py:12
  118.2 1.3 collective-permute-start.39
  119.5 4.0 collective-permute-start.34
  126.7 1.3 collective-permute-start.44
  128.8 5.9 %collective-permute-start.41 = (f32[2,16,8,1]{3,2,1,0:T(8,128)}, f32[2,16,8,1]{3,2,1,0:T(8,128)}, u32[]{:S(2)}, u32[]{:S(2)}) collective-permute-start(f32[2,16,8,1]{3,2,1,0:T(8,128)} %pad_maximum_fusion.1), channel_id=1, source_target_pairs={{0,1},{1,2},{2,3},{3,4},{4,5},{5,6},{6,7},{8,9},{9,10},{10,11},{11... | collective-permute-start | bytes 3080 | tf_op jit(solution)/shard_map/ppermute | solution.py:12
  136.0 3.2 collective-permute-start.43
  139.2 1.3 collective-permute-start.40
  143.6 15.1 %scatter_fusion.2 = f32[16,8,128]{2,1,0:T(8,128)S(1)} fusion(f32[16,8,128]{2,1,0:T(8,128)S(1)} %fusion.89, s32[256]{0:T(256)S(1)} %bitcast.388, f32[256]{0:T(256)S(1)} %bitcast.528), kind=kCustom, calls=%fused_computation.2 | custom fusion | flops 256 | bytes 6144 | tf_op jit(solution)/shard_map/scatter-add | solution.py:141
  159.6 1.8 add_bitcast_fusion
  163.9 3.9 collective-permute-start.5
  167.9 5.4 %collective-permute-start.45 = (f32[1,16,8,1]{3,2,1,0:T(8,128)}, f32[1,16,8,1]{3,2,1,0:T(8,128)}, u32[]{:S(2)}, u32[]{:S(2)}) collective-permute-start(f32[1,16,8,1]{3,2,1,0:T(8,128)} %slice.1308), channel_id=1, source_target_pairs={{0,1},{1,2},{2,3},{3,4},{4,5},{5,6},{6,7},{8,9},{9,10},{10,11},{11... | collective-permute-start | bytes 1544 | tf_op jit(solution)/shard_map/ppermute | solution.py:12
  173.9 4.0 collective-permute-start.42
  177.9 2.9 collective-permute-start.2
  180.9 1.3 collective-permute-start.7
  191.0 1.3 collective-permute-start.8
  198.7 1.2 fusion.147
  202.8 1.3 collective-permute-start.12
  205.5 1.3 collective-permute-start.46
  209.6 1.3 collective-permute-start.47
  210.9 1.2 fusion.146
  214.3 1.6 collective-permute-start.6
  218.4 1.3 fusion.95
  219.9 5.9 %collective-permute-start.9 = (f32[2,16,8,1]{3,1,2,0:T(8,128)S(1)}, f32[2,16,8,1]{3,1,2,0:T(8,128)S(1)}, u32[]{:S(2)}, u32[]{:S(2)}) collective-permute-start(f32[2,16,8,1]{3,1,2,0:T(8,128)S(1)} %pad_maximum_fusion.9), channel_id=1, source_target_pairs={{0,1},{1,2},{2,3},{3,4},{4,5},{5,6},{6,7},{8,9},{9,10},{10,11},{11... | collective-permute-start | bytes 3080 | tf_op jit(solution)/shard_map/ppermute | solution.py:12
  225.8 5.2 %collective-permute-start.11 = (f32[2,16,1,128]{3,1,2,0:T(8,128)S(1)}, f32[2,16,1,128]{3,1,2,0:T(8,128)S(1)}, u32[]{:S(2)}, u32[]{:S(2)}) collective-permute-start(f32[2,16,1,128]{3,1,2,0:T(8,128)S(1)} %pad_maximum_fusion.20), channel_id=1, source_target_pairs={{0,8},{8,16},{16,24},{1,9},{9,17},{17,25},{2,10},{10,18},{18,26},{... | collective-permute-start | bytes 49160 | tf_op jit(solution)/shard_map/ppermute | solution.py:12
  231.3 3.4 collective-permute-start.10
  236.0 3.4 collective-permute-start.13
  239.5 1.3 collective-permute-start.15
  240.8 1.3 collective-permute-start.16
  242.5 2.7 collective-permute-done.15
  245.6 1.1 fusion.150
  249.0 1.1 fusion.149
  252.4 1.3 collective-permute-start.20
  253.7 1.1 fusion.148
  257.0 1.3 collective-permute-start.14
  260.2 4.7 collective-permute-start.17
  264.9 4.0 collective-permute-start.19
  269.7 3.4 collective-permute-start.18
  273.5 3.5 collective-permute-start.21
  277.1 1.3 collective-permute-start.29
  278.4 1.3 collective-permute-start.28
  280.2 5.2 %collective-permute-done.28 = f32[2,16,8,1]{3,1,2,0:T(8,128)S(1)} collective-permute-done((f32[2,16,8,1]{3,1,2,0:T(8,128)S(1)}, f32[2,16,8,1]{3,1,2,0:T(8,128)S(1)}, u32[]{:S(2)}, u32[]{:S(2)}) %collective-permute-start.28) | collective-permute-done | bytes 1056 | tf_op jit(solution)/shard_map/ppermute | solution.py:12
  288.7 1.3 dynamic-slice.54
  290.0 198.0 %all-reduce.39.cloned.1.call-done = f32[3,16,8,128]{3,2,1,0:T(8,128)} async-done(((f32[3,16,8,128]{3,2,1,0:T(8,128)}), f32[3,16,8,128]{3,2,1,0:T(8,128)}) %all-reduce.39.cloned.1.call-update) | async-done | bytes 196624
  488.1 1.9 dynamic-slice_bitcast_fusion
  (414 shorter events, 67.1 us)
Async XLA Ops:
  7.2 480.9 %all-reduce.39.cloned.1.call-start = ((), (), s32[]{:S(2)}) async-start(), calls=%async_computation | async-start | bytes 393216
  8.3 5.5 %copy-start.3 = (bf16[1,9,16,8,128]{4,3,2,1,0:T(8,128)(2,1)S(1)}, bf16[1,9,16,8,128]{4,3,2,1,0:T(8,128)(2,1)}, u32[]{:S(2)}) copy-start(bf16[1,9,16,8,128]{4,3,2,1,0:T(8,128)(2,1)} %param.24) | copy-start | bytes 884740
  9.1 27.0 %collective-permute-start.23 = (f32[2,16,8,1]{3,1,2,0:T(8,128)}, f32[2,16,8,1]{3,1,2,0:T(8,128)}, u32[]{:S(2)}, u32[]{:S(2)}) collective-permute-start(f32[2,16,8,1]{3,1,2,0:T(8,128)} %pad_maximum_fusion.6), channel_id=1, source_target_pairs={{0,1},{1,2},{2,3},{3,4},{4,5},{5,6},{6,7},{8,9},{9,10},{10,11},{11... | collective-permute-start | bytes 3080 | tf_op jit(solution)/shard_map/ppermute | solution.py:12
  14.6 23.7 %collective-permute-start.1 = (f32[2,16,8,1]{3,1,2,0:T(8,128)}, f32[2,16,8,1]{3,1,2,0:T(8,128)}, u32[]{:S(2)}, u32[]{:S(2)}) collective-permute-start(f32[2,16,8,1]{3,1,2,0:T(8,128)} %pad_maximum_fusion.11), channel_id=1, source_target_pairs={{0,1},{1,2},{2,3},{3,4},{4,5},{5,6},{6,7},{8,9},{9,10},{10,11},{11... | collective-permute-start | bytes 3080 | tf_op jit(solution)/shard_map/ppermute | solution.py:12
  18.6 25.8 %collective-permute-start.25 = (f32[2,16,1,128]{3,1,2,0:T(8,128)S(1)}, f32[2,16,1,128]{3,1,2,0:T(8,128)S(1)}, u32[]{:S(2)}, u32[]{:S(2)}) collective-permute-start(f32[2,16,1,128]{3,1,2,0:T(8,128)S(1)} %slice.1229), channel_id=1, source_target_pairs={{0,8},{8,16},{16,24},{1,9},{9,17},{17,25},{2,10},{10,18},{18,26},{... | collective-permute-start | bytes 49160 | tf_op jit(solution)/shard_map/ppermute | solution.py:12
  22.5 21.9 %collective-permute-start = (f32[1,16,1,128]{3,1,2,0:T(8,128)}, f32[1,16,1,128]{3,1,2,0:T(8,128)S(1)}, u32[]{:S(2)}, u32[]{:S(2)}) collective-permute-start(f32[1,16,1,128]{3,1,2,0:T(8,128)} %bitcast.181), channel_id=1, source_target_pairs={{8,0},{16,8},{24,16},{9,1},{17,9},{25,17},{10,2},{18,10},{26,18},{... | collective-permute-start | bytes 24584 | tf_op jit(solution)/shard_map/ppermute | solution.py:12
  24.4 10.1 %collective-permute-start.4 = (f32[1,16,8,1]{3,2,1,0:T(8,128)}, f32[1,16,8,1]{3,2,1,0:T(8,128)S(1)}, u32[]{:S(2)}, u32[]{:S(2)}) collective-permute-start(f32[1,16,8,1]{3,2,1,0:T(8,128)} %slice.1144), channel_id=1, source_target_pairs={{1,0},{2,1},{3,2},{4,3},{5,4},{6,5},{7,6},{9,8},{10,9},{11,10},{12... | collective-permute-start | bytes 1544 | tf_op jit(solution)/shard_map/ppermute | solution.py:12
  34.6 10.7 %collective-permute-start.26 = (f32[1,16,8,1]{3,1,2,0:T(8,128)}, f32[1,16,8,1]{3,1,2,0:T(8,128)}, u32[]{:S(2)}, u32[]{:S(2)}) collective-permute-start(f32[1,16,8,1]{3,1,2,0:T(8,128)} %slice.1234), channel_id=1, source_target_pairs={{1,0},{2,1},{3,2},{4,3},{5,4},{6,5},{7,6},{9,8},{10,9},{11,10},{12... | collective-permute-start | bytes 1544 | tf_op jit(solution)/shard_map/ppermute | solution.py:12
  36.1 9.1 %collective-permute-start.22 = (f32[1,16,1,128]{3,1,2,0:T(8,128)}, f32[1,16,1,128]{3,1,2,0:T(8,128)S(1)}, u32[]{:S(2)}, u32[]{:S(2)}) collective-permute-start(f32[1,16,1,128]{3,1,2,0:T(8,128)} %slice.1219), channel_id=1, source_target_pairs={{8,0},{16,8},{24,16},{9,1},{17,9},{25,17},{10,2},{18,10},{26,18},{... | collective-permute-start | bytes 24584 | tf_op jit(solution)/shard_map/ppermute | solution.py:12
  38.3 25.1 %collective-permute-start.3 = (f32[2,16,1,128]{3,1,2,0:T(8,128)S(1)}, f32[2,16,1,128]{3,1,2,0:T(8,128)}, u32[]{:S(2)}, u32[]{:S(2)}) collective-permute-start(f32[2,16,1,128]{3,1,2,0:T(8,128)S(1)} %bitcast.515), channel_id=1, source_target_pairs={{0,8},{8,16},{16,24},{1,9},{9,17},{17,25},{2,10},{10,18},{18,26},{... | collective-permute-start | bytes 49160 | tf_op jit(solution)/shard_map/ppermute | solution.py:12
  62.1 13.8 %collective-permute-start.30 = (f32[2,16,8,1]{3,2,1,0:T(8,128)S(1)}, f32[2,16,8,1]{3,2,1,0:T(8,128)S(1)}, u32[]{:S(2)}, u32[]{:S(2)}) collective-permute-start(f32[2,16,8,1]{3,2,1,0:T(8,128)S(1)} %pad_maximum_fusion.4), channel_id=1, source_target_pairs={{1,0},{2,1},{3,2},{4,3},{5,4},{6,5},{7,6},{9,8},{10,9},{11,10},{12... | collective-permute-start | bytes 3080 | tf_op jit(solution)/shard_map/ppermute | solution.py:12
  65.3 11.2 %collective-permute-start.31 = (f32[2,16,1,128]{3,1,2,0:T(8,128)S(1)}, f32[2,16,1,128]{3,1,2,0:T(8,128)S(1)}, u32[]{:S(2)}, u32[]{:S(2)}) collective-permute-start(f32[2,16,1,128]{3,1,2,0:T(8,128)S(1)} %pad_maximum_fusion.16), channel_id=1, source_target_pairs={{8,0},{16,8},{24,16},{9,1},{17,9},{25,17},{10,2},{18,10},{26,18},{... | collective-permute-start | bytes 49160 | tf_op jit(solution)/shard_map/ppermute | solution.py:12
  66.6 10.6 %collective-permute-start.24 = (f32[1,16,1,128]{3,1,2,0:T(8,128)S(1)}, f32[1,16,1,128]{3,1,2,0:T(8,128)S(1)}, u32[]{:S(2)}, u32[]{:S(2)}) collective-permute-start(f32[1,16,1,128]{3,1,2,0:T(8,128)S(1)} %bitcast.525), channel_id=1, source_target_pairs={{0,8},{8,16},{16,24},{1,9},{9,17},{17,25},{2,10},{10,18},{18,26},{... | collective-permute-start | bytes 24584 | tf_op jit(solution)/shard_map/ppermute | solution.py:12
  70.6 6.6 %collective-permute-start.27 = (f32[1,16,8,1]{3,1,2,0:T(8,128)S(1)}, f32[1,16,8,1]{3,1,2,0:T(8,128)S(1)}, u32[]{:S(2)}, u32[]{:S(2)}) collective-permute-start(f32[1,16,8,1]{3,1,2,0:T(8,128)S(1)} %slice.1236), channel_id=1, source_target_pairs={{0,1},{1,2},{2,3},{3,4},{4,5},{5,6},{6,7},{8,9},{9,10},{10,11},{11... | collective-permute-start | bytes 1544 | tf_op jit(solution)/shard_map/ppermute | solution.py:12
  78.9 11.9 %collective-permute-start.35 = (f32[2,16,1,128]{3,1,2,0:T(8,128)S(1)}, f32[2,16,1,128]{3,1,2,0:T(8,128)S(1)}, u32[]{:S(2)}, u32[]{:S(2)}) collective-permute-start(f32[2,16,1,128]{3,1,2,0:T(8,128)S(1)} %pad_maximum_fusion.15), channel_id=1, source_target_pairs={{0,8},{8,16},{16,24},{1,9},{9,17},{17,25},{2,10},{10,18},{18,26},{... | collective-permute-start | bytes 49160 | tf_op jit(solution)/shard_map/ppermute | solution.py:12
  82.5 8.0 %collective-permute-start.33 = (f32[2,16,8,1]{3,1,2,0:T(8,128)S(1)}, f32[2,16,8,1]{3,1,2,0:T(8,128)S(1)}, u32[]{:S(2)}, u32[]{:S(2)}) collective-permute-start(f32[2,16,8,1]{3,1,2,0:T(8,128)S(1)} %pad_maximum_fusion.3), channel_id=1, source_target_pairs={{0,1},{1,2},{2,3},{3,4},{4,5},{5,6},{6,7},{8,9},{9,10},{10,11},{11... | collective-permute-start | bytes 3080 | tf_op jit(solution)/shard_map/ppermute | solution.py:12
  87.9 5.3 %collective-permute-start.36 = (f32[1,16,8,1]{3,1,2,0:T(8,128)S(1)}, f32[1,16,8,1]{3,1,2,0:T(8,128)S(1)}, u32[]{:S(2)}, u32[]{:S(2)}) collective-permute-start(f32[1,16,8,1]{3,1,2,0:T(8,128)S(1)} %bitcast.461), channel_id=1, source_target_pairs={{1,0},{2,1},{3,2},{4,3},{5,4},{6,5},{7,6},{9,8},{10,9},{11,10},{12... | collective-permute-start | bytes 1544 | tf_op jit(solution)/shard_map/ppermute | solution.py:12
  89.2 4.4 collective-permute-start.32
  93.2 0.9 slice-start
  110.8 13.0 %collective-permute-start.38 = (f32[2,16,8,1]{3,1,2,0:T(8,128)}, f32[2,16,8,1]{3,1,2,0:T(8,128)S(1)}, u32[]{:S(2)}, u32[]{:S(2)}) collective-permute-start(f32[2,16,8,1]{3,1,2,0:T(8,128)} %pad_maximum_fusion.2), channel_id=1, source_target_pairs={{1,0},{2,1},{3,2},{4,3},{5,4},{6,5},{7,6},{9,8},{10,9},{11,10},{12... | collective-permute-start | bytes 3080 | tf_op jit(solution)/shard_map/ppermute | solution.py:12
  112.2 11.3 %collective-permute-start.37 = (f32[1,16,8,1]{3,2,1,0:T(8,128)S(1)}, f32[1,16,8,1]{3,2,1,0:T(8,128)S(1)}, u32[]{:S(2)}, u32[]{:S(2)}) collective-permute-start(f32[1,16,8,1]{3,2,1,0:T(8,128)S(1)} %slice.1278), channel_id=1, source_target_pairs={{0,1},{1,2},{2,3},{3,4},{4,5},{5,6},{6,7},{8,9},{9,10},{10,11},{11... | collective-permute-start | bytes 1544 | tf_op jit(solution)/shard_map/ppermute | solution.py:12
  118.2 6.6 %collective-permute-start.39 = (f32[2,16,1,128]{3,1,2,0:T(8,128)S(1)}, f32[2,16,1,128]{3,1,2,0:T(8,128)S(1)}, u32[]{:S(2)}, u32[]{:S(2)}) collective-permute-start(f32[2,16,1,128]{3,1,2,0:T(8,128)S(1)} %pad_maximum_fusion.14), channel_id=1, source_target_pairs={{8,0},{16,8},{24,16},{9,1},{17,9},{25,17},{10,2},{18,10},{26,18},{... | collective-permute-start | bytes 49160 | tf_op jit(solution)/shard_map/ppermute | solution.py:12
  119.5 5.3 %collective-permute-start.34 = (f32[1,16,1,128]{3,1,2,0:T(8,128)S(1)}, f32[1,16,1,128]{3,1,2,0:T(8,128)S(1)}, u32[]{:S(2)}, u32[]{:S(2)}) collective-permute-start(f32[1,16,1,128]{3,1,2,0:T(8,128)S(1)} %slice.1271), channel_id=1, source_target_pairs={{0,8},{8,16},{16,24},{1,9},{9,17},{17,25},{2,10},{10,18},{18,26},{... | collective-permute-start | bytes 24584 | tf_op jit(solution)/shard_map/ppermute | solution.py:12
  126.7 13.9 %collective-permute-start.44 = (f32[1,16,8,1]{3,2,1,0:T(8,128)S(1)}, f32[1,16,8,1]{3,2,1,0:T(8,128)S(1)}, u32[]{:S(2)}, u32[]{:S(2)}) collective-permute-start(f32[1,16,8,1]{3,2,1,0:T(8,128)S(1)} %bitcast.473), channel_id=1, source_target_pairs={{1,0},{2,1},{3,2},{4,3},{5,4},{6,5},{7,6},{9,8},{10,9},{11,10},{12... | collective-permute-start | bytes 1544 | tf_op jit(solution)/shard_map/ppermute | solution.py:12
  128.8 12.7 %collective-permute-start.41 = (f32[2,16,8,1]{3,2,1,0:T(8,128)}, f32[2,16,8,1]{3,2,1,0:T(8,128)}, u32[]{:S(2)}, u32[]{:S(2)}) collective-permute-start(f32[2,16,8,1]{3,2,1,0:T(8,128)} %pad_maximum_fusion.1), channel_id=1, source_target_pairs={{0,1},{1,2},{2,3},{3,4},{4,5},{5,6},{6,7},{8,9},{9,10},{10,11},{11... | collective-permute-start | bytes 3080 | tf_op jit(solution)/shard_map/ppermute | solution.py:12
  136.0 7.5 %collective-permute-start.43 = (f32[2,16,1,128]{3,2,1,0:T(1,128)S(1)}, f32[2,16,1,128]{3,2,1,0:T(1,128)S(1)}, u32[]{:S(2)}, u32[]{:S(2)}) collective-permute-start(f32[2,16,1,128]{3,2,1,0:T(1,128)S(1)} %pad_maximum_fusion.13), channel_id=1, source_target_pairs={{0,8},{8,16},{16,24},{1,9},{9,17},{17,25},{2,10},{10,18},{18,26},{... | collective-permute-start | bytes 49160 | tf_op jit(solution)/shard_map/ppermute | solution.py:12
  139.2 19.5 %collective-permute-start.40 = (f32[1,16,1,128]{3,1,2,0:T(8,128)S(1)}, f32[1,16,1,128]{3,1,2,0:T(8,128)S(1)}, u32[]{:S(2)}, u32[]{:S(2)}) collective-permute-start(f32[1,16,1,128]{3,1,2,0:T(8,128)S(1)} %bitcast.526), channel_id=1, source_target_pairs={{8,0},{16,8},{24,16},{9,1},{17,9},{25,17},{10,2},{18,10},{26,18},{... | collective-permute-start | bytes 24584 | tf_op jit(solution)/shard_map/ppermute | solution.py:12
  143.6 15.2 %copy-start.25 = (f32[16,8,128]{2,0,1:T(8,128)S(1)}, f32[16,8,128]{2,0,1:T(8,128)}, u32[]{:S(2)}) copy-start(f32[16,8,128]{2,0,1:T(8,128)} %get-tuple-element.178) | copy-start | bytes 196612
  163.9 26.5 %collective-permute-start.5 = (f32[1,16,8,1]{3,2,1,0:T(8,128)S(1)}, f32[1,16,8,1]{3,2,1,0:T(8,128)S(1)}, u32[]{:S(2)}, u32[]{:S(2)}) collective-permute-start(f32[1,16,8,1]{3,2,1,0:T(8,128)S(1)} %slice.1146), channel_id=1, source_target_pairs={{0,1},{1,2},{2,3},{3,4},{4,5},{5,6},{6,7},{8,9},{9,10},{10,11},{11... | collective-permute-start | bytes 1544 | tf_op jit(solution)/shard_map/ppermute | solution.py:12
  167.9 25.6 %collective-permute-start.45 = (f32[1,16,8,1]{3,2,1,0:T(8,128)}, f32[1,16,8,1]{3,2,1,0:T(8,128)}, u32[]{:S(2)}, u32[]{:S(2)}) collective-permute-start(f32[1,16,8,1]{3,2,1,0:T(8,128)} %slice.1308), channel_id=1, source_target_pairs={{0,1},{1,2},{2,3},{3,4},{4,5},{5,6},{6,7},{8,9},{9,10},{10,11},{11... | collective-permute-start | bytes 1544 | tf_op jit(solution)/shard_map/ppermute | solution.py:12
  173.9 23.3 %collective-permute-start.42 = (f32[1,16,1,128]{3,1,2,0:T(8,128)}, f32[1,16,1,128]{3,1,2,0:T(8,128)S(1)}, u32[]{:S(2)}, u32[]{:S(2)}) collective-permute-start(f32[1,16,1,128]{3,1,2,0:T(8,128)} %slice.1301), channel_id=1, source_target_pairs={{0,8},{8,16},{16,24},{1,9},{9,17},{17,25},{2,10},{10,18},{18,26},{... | collective-permute-start | bytes 24584 | tf_op jit(solution)/shard_map/ppermute | solution.py:12
  177.9 19.2 %collective-permute-start.2 = (f32[1,16,1,128]{3,1,2,0:T(8,128)S(1)}, f32[1,16,1,128]{3,1,2,0:T(8,128)S(1)}, u32[]{:S(2)}, u32[]{:S(2)}) collective-permute-start(f32[1,16,1,128]{3,1,2,0:T(8,128)S(1)} %bitcast.524), channel_id=1, source_target_pairs={{0,8},{8,16},{16,24},{1,9},{9,17},{17,25},{2,10},{10,18},{18,26},{... | collective-permute-start | bytes 24584 | tf_op jit(solution)/shard_map/ppermute | solution.py:12
  180.9 13.6 %collective-permute-start.7 = (f32[2,16,8,1]{3,2,1,0:T(8,128)}, f32[2,16,8,1]{3,2,1,0:T(8,128)}, u32[]{:S(2)}, u32[]{:S(2)}) collective-permute-start(f32[2,16,8,1]{3,2,1,0:T(8,128)} %pad_maximum_fusion.10), channel_id=1, source_target_pairs={{1,0},{2,1},{3,2},{4,3},{5,4},{6,5},{7,6},{9,8},{10,9},{11,10},{12... | collective-permute-start | bytes 3080 | tf_op jit(solution)/shard_map/ppermute | solution.py:12
  191.0 26.5 %collective-permute-start.8 = (f32[2,16,1,128]{3,1,2,0:T(8,128)}, f32[2,16,1,128]{3,1,2,0:T(8,128)}, u32[]{:S(2)}, u32[]{:S(2)}) collective-permute-start(f32[2,16,1,128]{3,1,2,0:T(8,128)} %pad_maximum_fusion.21), channel_id=1, source_target_pairs={{8,0},{16,8},{24,16},{9,1},{17,9},{25,17},{10,2},{18,10},{26,18},{... | collective-permute-start | bytes 49160 | tf_op jit(solution)/shard_map/ppermute | solution.py:12
  202.0 2.0 copy-start.19
  202.8 32.0 %collective-permute-start.12 = (f32[1,16,8,1]{3,1,2,0:T(8,128)S(1)}, f32[1,16,8,1]{3,1,2,0:T(8,128)}, u32[]{:S(2)}, u32[]{:S(2)}) collective-permute-start(f32[1,16,8,1]{3,1,2,0:T(8,128)S(1)} %bitcast.460), channel_id=1, source_target_pairs={{1,0},{2,1},{3,2},{4,3},{5,4},{6,5},{7,6},{9,8},{10,9},{11,10},{12... | collective-permute-start | bytes 1544 | tf_op jit(solution)/shard_map/ppermute | solution.py:12
  205.5 11.1 %collective-permute-start.46 = (f32[2,16,8,1]{3,1,2,0:T(8,128)S(1)}, f32[2,16,8,1]{3,1,2,0:T(8,128)}, u32[]{:S(2)}, u32[]{:S(2)}) collective-permute-start(f32[2,16,8,1]{3,1,2,0:T(8,128)S(1)} %pad_maximum_fusion), channel_id=1, source_target_pairs={{1,0},{2,1},{3,2},{4,3},{5,4},{6,5},{7,6},{9,8},{10,9},{11,10},{12... | collective-permute-start | bytes 3080 | tf_op jit(solution)/shard_map/ppermute | solution.py:12
  209.6 6.4 %copy-start.17 = (f32[1,16,8,128]{3,1,2,0:T(8,128)S(1)}, f32[1,16,8,128]{3,1,2,0:T(8,128)}, u32[]{:S(2)}) copy-start(f32[1,16,8,128]{3,1,2,0:T(8,128)} %get-tuple-element.77) | copy-start | bytes 196612
  209.6 8.7 %collective-permute-start.47 = (f32[2,16,1,128]{3,1,2,0:T(8,128)S(1)}, f32[2,16,1,128]{3,1,2,0:T(8,128)S(1)}, u32[]{:S(2)}, u32[]{:S(2)}) collective-permute-start(f32[2,16,1,128]{3,1,2,0:T(8,128)S(1)} %pad_maximum_fusion.12), channel_id=1, source_target_pairs={{8,0},{16,8},{24,16},{9,1},{17,9},{25,17},{10,2},{18,10},{26,18},{... | collective-permute-start | bytes 49160 | tf_op jit(solution)/shard_map/ppermute | solution.py:12
  214.3 4.1 copy-start.15
  214.3 4.1 copy-start.16
  214.3 16.7 %collective-permute-start.6 = (f32[1,16,1,128]{3,1,2,0:T(8,128)S(1)}, f32[1,16,1,128]{3,1,2,0:T(8,128)S(1)}, u32[]{:S(2)}, u32[]{:S(2)}) collective-permute-start(f32[1,16,1,128]{3,1,2,0:T(8,128)S(1)} %slice.1157), channel_id=1, source_target_pairs={{8,0},{16,8},{24,16},{9,1},{17,9},{25,17},{10,2},{18,10},{26,18},{... | collective-permute-start | bytes 24584 | tf_op jit(solution)/shard_map/ppermute | solution.py:12
  216.0 2.4 copy-start.13
  216.0 2.4 copy-start.14
  216.6 1.8 copy-start.8
  216.6 1.8 copy-start.9
  216.6 1.8 copy-start.10
  216.6 1.8 copy-start.11
  219.9 11.2 %collective-permute-start.9 = (f32[2,16,8,1]{3,1,2,0:T(8,128)S(1)}, f32[2,16,8,1]{3,1,2,0:T(8,128)S(1)}, u32[]{:S(2)}, u32[]{:S(2)}) collective-permute-start(f32[2,16,8,1]{3,1,2,0:T(8,128)S(1)} %pad_maximum_fusion.9), channel_id=1, source_target_pairs={{0,1},{1,2},{2,3},{3,4},{4,5},{5,6},{6,7},{8,9},{9,10},{10,11},{11... | collective-permute-start | bytes 3080 | tf_op jit(solution)/shard_map/ppermute | solution.py:12
  225.8 8.9 %collective-permute-start.11 = (f32[2,16,1,128]{3,1,2,0:T(8,128)S(1)}, f32[2,16,1,128]{3,1,2,0:T(8,128)S(1)}, u32[]{:S(2)}, u32[]{:S(2)}) collective-permute-start(f32[2,16,1,128]{3,1,2,0:T(8,128)S(1)} %pad_maximum_fusion.20), channel_id=1, source_target_pairs={{0,8},{8,16},{16,24},{1,9},{9,17},{17,25},{2,10},{10,18},{18,26},{... | collective-permute-start | bytes 49160 | tf_op jit(solution)/shard_map/ppermute | solution.py:12
  231.3 3.4 copy-start.12
  231.3 13.9 %collective-permute-start.10 = (f32[1,16,1,128]{3,1,2,0:T(8,128)S(1)}, f32[1,16,1,128]{3,1,2,0:T(8,128)S(1)}, u32[]{:S(2)}, u32[]{:S(2)}) collective-permute-start(f32[1,16,1,128]{3,1,2,0:T(8,128)S(1)} %slice.1171), channel_id=1, source_target_pairs={{0,8},{8,16},{16,24},{1,9},{9,17},{17,25},{2,10},{10,18},{18,26},{... | collective-permute-start | bytes 24584 | tf_op jit(solution)/shard_map/ppermute | solution.py:12
  236.0 6.1 %collective-permute-start.13 = (f32[1,16,8,1]{3,2,1,0:T(8,128)S(1)}, f32[1,16,8,1]{3,2,1,0:T(8,128)S(1)}, u32[]{:S(2)}, u32[]{:S(2)}) collective-permute-start(f32[1,16,8,1]{3,2,1,0:T(8,128)S(1)} %slice.1178), channel_id=1, source_target_pairs={{0,1},{1,2},{2,3},{3,4},{4,5},{5,6},{6,7},{8,9},{9,10},{10,11},{11... | collective-permute-start | bytes 1544 | tf_op jit(solution)/shard_map/ppermute | solution.py:12
  239.5 5.7 %collective-permute-start.15 = (f32[2,16,8,1]{3,1,2,0:T(8,128)S(1)}, f32[2,16,8,1]{3,1,2,0:T(8,128)S(1)}, u32[]{:S(2)}, u32[]{:S(2)}) collective-permute-start(f32[2,16,8,1]{3,1,2,0:T(8,128)S(1)} %pad_maximum_fusion.8), channel_id=1, source_target_pairs={{1,0},{2,1},{3,2},{4,3},{5,4},{6,5},{7,6},{9,8},{10,9},{11,10},{12... | collective-permute-start | bytes 3080 | tf_op jit(solution)/shard_map/ppermute | solution.py:12
  240.8 18.3 %collective-permute-start.16 = (f32[2,16,1,128]{3,1,2,0:T(8,128)S(1)}, f32[2,16,1,128]{3,1,2,0:T(8,128)S(1)}, u32[]{:S(2)}, u32[]{:S(2)}) collective-permute-start(f32[2,16,1,128]{3,1,2,0:T(8,128)S(1)} %pad_maximum_fusion.19), channel_id=1, source_target_pairs={{8,0},{16,8},{24,16},{9,1},{17,9},{25,17},{10,2},{18,10},{26,18},{... | collective-permute-start | bytes 49160 | tf_op jit(solution)/shard_map/ppermute | solution.py:12
  252.4 6.5 %collective-permute-start.20 = (f32[1,16,8,1]{3,2,1,0:T(8,128)S(1)}, f32[1,16,8,1]{3,2,1,0:T(8,128)S(1)}, u32[]{:S(2)}, u32[]{:S(2)}) collective-permute-start(f32[1,16,8,1]{3,2,1,0:T(8,128)S(1)} %bitcast.466), channel_id=1, source_target_pairs={{1,0},{2,1},{3,2},{4,3},{5,4},{6,5},{7,6},{9,8},{10,9},{11,10},{12... | collective-permute-start | bytes 1544 | tf_op jit(solution)/shard_map/ppermute | solution.py:12
  257.0 12.3 %collective-permute-start.14 = (f32[1,16,1,128]{3,1,2,0:T(8,128)S(1)}, f32[1,16,1,128]{3,1,2,0:T(8,128)S(1)}, u32[]{:S(2)}, u32[]{:S(2)}) collective-permute-start(f32[1,16,1,128]{3,1,2,0:T(8,128)S(1)} %slice.1187), channel_id=1, source_target_pairs={{8,0},{16,8},{24,16},{9,1},{17,9},{25,17},{10,2},{18,10},{26,18},{... | collective-permute-start | bytes 24584 | tf_op jit(solution)/shard_map/ppermute | solution.py:12
  260.2 8.8 %collective-permute-start.17 = (f32[2,16,8,1]{3,2,1,0:T(8,128)S(1)}, f32[2,16,8,1]{3,2,1,0:T(8,128)S(1)}, u32[]{:S(2)}, u32[]{:S(2)}) collective-permute-start(f32[2,16,8,1]{3,2,1,0:T(8,128)S(1)} %pad_maximum_fusion.7), channel_id=1, source_target_pairs={{0,1},{1,2},{2,3},{3,4},{4,5},{5,6},{6,7},{8,9},{9,10},{10,11},{11... | collective-permute-start | bytes 3080 | tf_op jit(solution)/shard_map/ppermute | solution.py:12
  264.9 8.2 %collective-permute-start.19 = (f32[2,16,1,128]{3,2,1,0:T(1,128)S(1)}, f32[2,16,1,128]{3,2,1,0:T(1,128)S(1)}, u32[]{:S(2)}, u32[]{:S(2)}) collective-permute-start(f32[2,16,1,128]{3,2,1,0:T(1,128)S(1)} %pad_maximum_fusion.18), channel_id=1, source_target_pairs={{0,8},{8,16},{16,24},{1,9},{9,17},{17,25},{2,10},{10,18},{18,26},{... | collective-permute-start | bytes 49160 | tf_op jit(solution)/shard_map/ppermute | solution.py:12
  269.7 10.3 %collective-permute-start.18 = (f32[1,16,1,128]{3,1,2,0:T(8,128)S(1)}, f32[1,16,1,128]{3,1,2,0:T(8,128)S(1)}, u32[]{:S(2)}, u32[]{:S(2)}) collective-permute-start(f32[1,16,1,128]{3,1,2,0:T(8,128)S(1)} %slice.1201), channel_id=1, source_target_pairs={{0,8},{8,16},{16,24},{1,9},{9,17},{17,25},{2,10},{10,18},{18,26},{... | collective-permute-start | bytes 24584 | tf_op jit(solution)/shard_map/ppermute | solution.py:12
  273.5 6.3 %collective-permute-start.21 = (f32[1,16,8,1]{3,2,1,0:T(8,128)S(1)}, f32[1,16,8,1]{3,2,1,0:T(8,128)S(1)}, u32[]{:S(2)}, u32[]{:S(2)}) collective-permute-start(f32[1,16,8,1]{3,2,1,0:T(8,128)S(1)} %slice.1208), channel_id=1, source_target_pairs={{0,1},{1,2},{2,3},{3,4},{4,5},{5,6},{6,7},{8,9},{9,10},{10,11},{11... | collective-permute-start | bytes 1544 | tf_op jit(solution)/shard_map/ppermute | solution.py:12
  277.1 8.5 %collective-permute-start.29 = (f32[2,16,1,128]{3,1,2,0:T(8,128)S(1)}, f32[2,16,1,128]{3,1,2,0:T(8,128)S(1)}, u32[]{:S(2)}, u32[]{:S(2)}) collective-permute-start(f32[2,16,1,128]{3,1,2,0:T(8,128)S(1)} %pad_maximum_fusion.17), channel_id=1, source_target_pairs={{8,0},{16,8},{24,16},{9,1},{17,9},{25,17},{10,2},{18,10},{26,18},{... | collective-permute-start | bytes 49160 | tf_op jit(solution)/shard_map/ppermute | solution.py:12
  278.4 6.9 %collective-permute-start.28 = (f32[2,16,8,1]{3,1,2,0:T(8,128)S(1)}, f32[2,16,8,1]{3,1,2,0:T(8,128)S(1)}, u32[]{:S(2)}, u32[]{:S(2)}) collective-permute-start(f32[2,16,8,1]{3,1,2,0:T(8,128)S(1)} %pad_maximum_fusion.5), channel_id=1, source_target_pairs={{1,0},{2,1},{3,2},{4,3},{5,4},{6,5},{7,6},{9,8},{10,9},{11,10},{12... | collective-permute-start | bytes 3080 | tf_op jit(solution)/shard_map/ppermute | solution.py:12
  287.1 0.9 copy-start.26
  (21 other events, 16.1 us)
Sparse Core Ops, SparseCore 0:
  288.9 199.1 all-reduce.38
where the time goes:
time: 500 us; the launch traced here: 497 us
  waiting for transfers between devices  210 us (42%)
  starting transfers between devices  133 us (27%)
  other arithmetic  72.1 us (14%)
  local copies, waits for them, and re-layouts  50.6 us (10%)
  between operations  30.7 us (6%)
    unnamed x2, waiting for transfers between devices  198 us
    ppermute x48, starting transfers between devices, from_behind(): lax.ppermute(value, axis, [(source, source + steps) for source in range(f...  133 us
    scatter-add x3, other arithmetic, inject(): return field.at[depth, local_x, local_y].add(values, mode='drop')  45.3 us
    unnamed x108, local copies, waits for them, and re-layouts  19.9 us
    ppermute x48, waiting for transfers between devices, from_behind(): lax.ppermute(value, axis, [(source, source + steps) for source in range(f...  12 us
  transfers between devices with their start and end apart: 49, of which 7 were waited for; matrix products, arithmetic and copies ran while one was open for 17% of the time, Pallas kernels for 0%

commit v1 on v0

v1 whole, which is shorter than its diff:
```python
import jax
import jax.numpy as jnp
from jax import lax
from jax.experimental import pallas as pl
from jax.experimental.pallas import tpu as pltpu
from jax.sharding import PartitionSpec as P

courant = 0.2
HALO = 3
MESH = pl.DeviceIdType.MESH
CORES, RING, HALVES = 2, 4, 2


def kernel(
    gx_tiles, gy_tiles, steps,
    states, mats, wavelet, source_x, source_y, aperture, residual, receiver_x, receiver_y,
    out_lambda, out_mu, out_rho,
    field, model, x_low, x_high, m_low, m_high, pack, pack_low, pack_high,
    strain, motion, lifted, term, chunks, got_core, sum_core, got_ring, sum_ring, got_half,
    send, recv,
):
    fields2, cx, nz, cy = states.shape
    runs = fields2 // 9
    wide = cx + 2 * HALO
    gx, gy, shot = lax.axis_index("gx"), lax.axis_index("gy"), lax.axis_index("shot")
    half, ring, core = shot // (RING * CORES), lax.rem(shot // CORES, RING), lax.rem(shot, CORES)
    x_start, y_start = gx * cx, gy * cy

    def there(dx, dy):
        ok = None
        for delta, at, count in ((dx, gx, gx_tiles), (dy, gy, gy_tiles)):
            if delta:
                one = at > 0 if delta < 0 else at < count - 1
                ok = one if ok is None else jnp.logical_and(ok, one)
        return ok

    def tile(dx, dy):
        return {"gx": gx + dx, "gy": gy + dy}

    near = [(dx, dy) for dx in (-1, 0, 1) for dy in (-1, 0, 1) if dx or dy]

    def shot_at(h, q, c):
        return {"shot": (h * RING + q) * CORES + c}

    peers = [shot_at(half, ring, 1 - core)]
    peers += [shot_at(half, lax.rem(ring + d, RING), core) for d in range(1, RING)]
    peers += [shot_at(1 - half, ring, core)]

    barrier = pltpu.get_barrier_semaphore()
    for peer in peers:
        pl.semaphore_signal(barrier, inc=1, device_id=peer, device_id_type=MESH)
    for dx, dy in near:
        @pl.when(there(dx, dy))
        def _():
            pl.semaphore_signal(barrier, inc=1, device_id=tile(dx, dy), device_id_type=MESH)

    lane = lax.broadcasted_iota(jnp.int32, (nz, cy), 1)

    def pack_row(x, carry):
        total = jnp.zeros((nz, cy), jnp.float32)
        for f in range(fields2 + 3):
            value = states[f, x].astype(jnp.float32) if f < fields2 else mats[f - fields2, x]
            moved = pltpu.roll(value, 6 * f + 3, axis=1)
            total = jnp.where((lane >= 6 * f) & (lane < 6 * f + 6), moved, total)
        pack[x] = total
        return carry

    lax.fori_loop(0, cx, pack_row, 0)

    along_x = jnp.minimum(gx, 1) + jnp.minimum(gx_tiles - 1 - gx, 1) + 1
    along_y = jnp.minimum(gy, 1) + jnp.minimum(gy_tiles - 1 - gy, 1) + 1
    pl.semaphore_wait(barrier, along_x * along_y - 1 + len(peers))

    def edge(dx):
        return pl.ds(0, HALO) if dx < 0 else pl.ds(cx - HALO, HALO)

    messages = []

    def message(dx, dy, source, target):
        n = len(messages)
        messages.append((dx, dy, pltpu.make_async_remote_copy(
            src_ref=source, dst_ref=target, send_sem=send.at[n], recv_sem=recv.at[n],
            device_id=tile(dx, dy), device_id_type=MESH)))

    for dx in (-1, 1):
        message(dx, 0, mats.at[:, edge(dx)], m_high if dx < 0 else m_low)
    for dx in (-1, 0, 1):
        for dy in (-1, 1):
            side = pack_high if dy < 0 else pack_low
            if dx == 0:
                message(dx, dy, pack, side.at[pl.ds(HALO, cx)])
            else:
                row = HALO + cx if dx < 0 else 0
                message(dx, dy, pack.at[edge(dx)], side.at[pl.ds(row, HALO)])
    shared = len(messages)
    for run in range(runs):
        for dx in (-1, 1):
            side = x_high if dx < 0 else x_low
            message(dx, 0, states.at[pl.ds(9 * run, 9), edge(dx)], side.at[run])
    order = list(range(shared + 2)) + list(range(shared + 2, len(messages)))
    for n in order:
        dx, dy, copy = messages[n]
        @pl.when(there(dx, dy))
        def _():
            copy.start()

    def blank(dx, dy, ref):
        @pl.when(jnp.logical_not(there(dx, dy)))
        def _():
            ref[...] = jnp.zeros(ref.shape, ref.dtype)

    for dx, side, model_side in ((-1, x_low, m_low), (1, x_high, m_high)):
        blank(dx, 0, side)
        blank(dx, 0, model_side)
    for dx in (-1, 0, 1):
        for dy, side in ((-1, pack_low), (1, pack_high)):
            row, count = {-1: (0, HALO), 0: (HALO, cx), 1: (HALO + cx, HALO)}[dx]
            blank(dx, dy, side.at[pl.ds(row, count)])

    def own_row(x, carry):
        for f in range(fields2):
            field[f, x + HALO, :, 0:cy] = states[f, x].astype(jnp.float32)
        for f in range(3):
            model[f, x + HALO, :, 0:cy] = mats[f, x]
        return carry

    lax.fori_loop(0, cx, own_row, 0)

    lanes2 = lax.broadcasted_iota(jnp.int32, (nz, 2 * cy), 1)
    depth = lax.broadcasted_iota(jnp.int32, (nz, 2 * cy), 0)
    column = jnp.where(lanes2 < cy + cy // 2, lanes2, lanes2 - 2 * cy) + y_start

    receivers = receiver_x.shape[1]
    rows = lax.broadcasted_iota(jnp.int32, (16, receivers), 0) + (x_start - HALO)
    hit_x = rows == receiver_x[...]
    cells = lax.broadcasted_iota(jnp.int32, (2 * cy, receivers), 0)
    cells = jnp.where(cells < cy + cy // 2, cells, cells - 2 * cy) + y_start
    hit_y = jnp.where(cells == receiver_y[...], 1.0, 0.0).astype(jnp.float32)
    for n in range(steps):
        picked = jnp.where(hit_x, residual[n : n + 1, :], 0.0)
        lifted[n] = lax.dot_general(
            picked, hit_y, (((1,), (1,)), ((), ())),
            precision=lax.Precision.HIGHEST, preferred_element_type=jnp.float32)

    def wait_recv(n):
        dx, dy, copy = messages[n]
        @pl.when(there(-dx, -dy))
        def _():
            copy.wait_recv()

    lane6 = lax.rem(lane, 6)
    at_edge = (lane < HALO) | (lane >= cy - HALO)

    def unpack_rows():
        def body(x, carry):
            both = jnp.where(lane6 < 3, pack_low[x], pack_high[x])
            for f in range(fields2 + 3):
                moved = pltpu.roll(both, (cy - HALO - 6 * f) % cy, axis=1)
                moved = jnp.where(at_edge, moved, 0.0)
                if f < fields2:
                    field[f, x, :, cy : 2 * cy] = moved
                else:
                    model[f - fields2, x, :, cy : 2 * cy] = moved
            return carry
        lax.fori_loop(0, wide, body, 0)

    def x_halo(run):
        for x in range(HALO):
            def body(f, carry):
                field[9 * run + f, x, :, 0:cy] = x_low[run, f, x].astype(jnp.float32)
                field[9 * run + f, HALO + cx + x, :, 0:cy] = x_high[run, f, x].astype(jnp.float32)
                return carry
            lax.fori_loop(0, 9, body, 0)

    for n in range(shared):
        wait_recv(n)
    for f in range(3):
        for x in range(HALO):
            model[f, x, :, 0:cy] = m_low[f, x]
            model[f, HALO + cx + x, :, 0:cy] = m_high[f, x]
    unpack_rows()

    first_z, last_z = depth == 0, depth == nz - 1

    def y_next(v):
        return pltpu.roll(v, 2 * cy - 1, axis=1)

    def y_back(v):
        return pltpu.roll(v, 1, axis=1)

    def z_next(v):
        return jnp.where(last_z, 0.0, pltpu.roll(v, nz - 1, axis=0))

    def z_back(v):
        return jnp.where(first_z, 0.0, pltpu.roll(v, 1, axis=0))

    pulse_at = jnp.where((depth == 2) & (column == source_y[0]), 1.0, 0.0).astype(jnp.float32)
    lift_at = depth == 1

    for run in range(runs):
        for n in (shared + 2 * run, shared + 2 * run + 1):
            wait_recv(n)
        x_halo(run)
        vx, vy, vz, sxx, syy, szz, sxy, sxz, syz = range(9 * run, 9 * run + 9)
        for n in range(steps):
            def velocity(j, carry):
                k = j + 1
                b0, b1 = model[2, j], model[2, k]
                xy0, xy1, xz0, xz1 = field[sxy, j], field[sxy, k], field[sxz, j], field[sxz, k]
                yy, zz, yz = field[syy, k], field[szz, k], field[syz, k]
                gain_x = b0 * ((field[sxx, k] - field[sxx, j]) + (xy0 - y_back(xy0)) + (xz0 - z_back(xz0)))
                gain_y = b1 * ((xy1 - xy0) + (y_next(yy) - yy) + (yz - z_back(yz)))
                gain_z = b1 * ((xz1 - xz0) + (yz - y_back(yz)) + (z_next(zz) - zz))
                new_x, new_y = field[vx, j] + gain_x, field[vy, k] + gain_y
                new_z = field[vz, k] + gain_z
                if run == 1:
                    row = lifted[steps - 1 - n, pl.ds(k, 1), :]
                    new_z = new_z + jnp.where(lift_at, row, 0.0)
                field[vx, j], field[vy, k], field[vz, k] = new_x, new_y, new_z
                if run == 0:
                    saved = (gain_x * (1.0 / courant), gain_y * (1.0 / courant), gain_z * (1.0 / courant))
                else:
                    saved = (new_x, new_y, new_z)
                motion[run, n, 0, j] = saved[0][:, 0:cy]
                motion[run, n, 1, k] = saved[1][:, 0:cy]
                motion[run, n, 2, k] = saved[2][:, 0:cy]
                return carry

            lax.fori_loop(n, wide - 1 - n, velocity, 0)

            def stress(k, carry):
                x0, y0, z0 = field[vx, k], field[vy, k], field[vz, k]
                e = (
                    x0 - field[vx, k - 1],
                    y0 - y_back(y0),
                    z0 - z_back(z0),
                    (y_next(x0) - x0) + (field[vy, k + 1] - y0),
                    (z_next(x0) - x0) + (field[vz, k + 1] - z0),
                    (z_next(y0) - y0) + (y_next(z0) - z0),
                )
                for c in range(6):
                    strain[run, n, c, k] = e[c][:, 0:cy]
                if n < steps - 1:
                    scaled = courant * model[1, k]
                    bulk = courant * model[0, k] * (e[0] + e[1] + e[2])
                    if run == 0:
                        amount = jnp.where(x_start + k - HALO == source_x[0], wavelet[0, n], 0.0)
                        bulk = bulk + amount * pulse_at
                    for c in range(3):
                        field[sxx + c, k] = field[sxx + c, k] + (bulk + 2.0 * scaled * e[c])
                    for c in range(3, 6):
                        field[sxx + c, k] = field[sxx + c, k] + scaled * e[c]
                return carry

            lax.fori_loop(n + 1, wide - 1 - n, stress, 0)

    factor = (-courant / (HALVES * RING * CORES)) * aperture[0].astype(jnp.float32)

    def image(x, carry):
        k = x + HALO
        first = second = third = jnp.zeros((nz, cy), jnp.float32)
        for m in range(steps):
            n = steps - 1 - m
            e = [strain[0, n, c, k] for c in range(6)]
            f = [strain[1, m, c, k] for c in range(6)]
            first = first + (e[0] + e[1] + e[2]) * (f[0] + f[1] + f[2])
            second = second + 2.0 * (e[0] * f[0] + e[1] * f[1] + e[2] * f[2])
            second = second + e[3] * f[3] + e[4] * f[4] + e[5] * f[5]
            for c in range(3):
                third = third + motion[0, n, c, k] * motion[1, m, c, k]
        term[0, x], term[1, x], term[2, x] = factor * first, factor * second, factor * third
        return carry

    lax.fori_loop(0, cx, image, 0)

    for t in range(3):
        turned = jnp.swapaxes(term[t], 0, 1)
        for z in range(nz):
            chunks[z % CORES, z // (CORES * RING), (z // CORES) % RING, t] = turned[z]

    base = len(messages)
    copy = pltpu.make_async_remote_copy(
        src_ref=chunks.at[1 - core], dst_ref=got_core, send_sem=send.at[base], recv_sem=recv.at[base],
        device_id=peers[0], device_id_type=MESH)
    copy.start()
    copy.wait_recv()
    last = [copy]
    sum_core[...] = chunks[core] + got_core[...]
    rings = []
    for d in range(1, RING):
        copy = pltpu.make_async_remote_copy(
            src_ref=sum_core.at[:, lax.rem(ring + d, RING)], dst_ref=got_ring.at[d - 1],
            send_sem=send.at[base + d], recv_sem=recv.at[base + d],
            device_id=peers[d], device_id_type=MESH)
        copy.start()
        rings.append(copy)
    total = sum_core[:, ring]
    for d in range(1, RING):
        rings[d - 1].wait_recv()
        total = total + got_ring[d - 1]
    sum_ring[...] = total
    copy = pltpu.make_async_remote_copy(
        src_ref=sum_ring.at[1 - half], dst_ref=got_half,
        send_sem=send.at[base + RING], recv_sem=recv.at[base + RING],
        device_id=peers[RING], device_id_type=MESH)
    copy.start()
    copy.wait_recv()
    last += rings + [copy]
    result = sum_ring[half] + got_half[...]
    out_lambda[0], out_mu[0], out_rho[0] = result[0], result[1], result[2]
    for copy in last:
        copy.wait_send()
    for dx, dy, copy in messages:
        @pl.when(there(dx, dy))
        def _():
            copy.wait_send()


def solution(mesh):
    gx_tiles, gy_tiles = mesh.shape["gx"], mesh.shape["gy"]

    def local(
        forward_state, adjoint_state, lame, shear, density, wavelet, residual,
        source_x, source_y, receiver_x, receiver_y, aperture,
    ):
        nz, cx, cy = lame.shape
        steps = wavelet.shape[1]
        wide = cx + 2 * HALO
        states = jnp.concatenate([forward_state[0], adjoint_state[0]]).swapaxes(1, 2)
        mats = jnp.stack([lame, shear, courant * (1.0 / density)]).swapaxes(1, 2)
        f32 = jnp.float32
        out = jax.ShapeDtypeStruct((1, cx, cy), f32)
        vmem = pl.BlockSpec(memory_space=pltpu.VMEM)
        smem = pl.BlockSpec(memory_space=pltpu.SMEM)
        V = pltpu.VMEM
        call = pl.pallas_call(
            lambda *refs: kernel(gx_tiles, gy_tiles, steps, *refs),
            out_shape=(out, out, out),
            in_specs=[vmem, vmem, smem, smem, smem, smem, vmem, vmem, vmem],
            out_specs=(vmem, vmem, vmem),
            scratch_shapes=[
                V((18, wide, nz, 2 * cy), f32),
                V((3, wide, nz, 2 * cy), f32),
                V((2, 9, HALO, nz, cy), jnp.bfloat16),
                V((2, 9, HALO, nz, cy), jnp.bfloat16),
                V((3, HALO, nz, cy), f32),
                V((3, HALO, nz, cy), f32),
                V((cx, nz, cy), f32),
                V((wide, nz, cy), f32),
                V((wide, nz, cy), f32),
                V((2, steps, 6, wide, nz, cy), f32),
                V((2, steps, 3, wide, nz, cy), f32),
                V((steps, 16, 2 * cy), f32),
                V((3, cx, nz, cy), f32),
                V((CORES, HALVES, RING, 3, cx, cy), f32),
                V((HALVES, RING, 3, cx, cy), f32),
                V((HALVES, RING, 3, cx, cy), f32),
                V((RING - 1, HALVES, 3, cx, cy), f32),
                V((HALVES, 3, cx, cy), f32),
                V((3, cx, cy), f32),
                pltpu.SemaphoreType.DMA((17,)),
                pltpu.SemaphoreType.DMA((17,)),
            ],
            compiler_params=pltpu.CompilerParams(collective_id=0, has_side_effects=True),
        )
        return call(
            states, mats, wavelet, source_x, source_y, aperture.reshape(1),
            residual[0], receiver_x, receiver_y,
        )

    return jax.shard_map(
        local,
        mesh=mesh,
        in_specs=(
            P("shot", None, None, "gx", "gy"),
            P("shot", None, None, "gx", "gy"),
            P(None, "gx", "gy"),
            P(None, "gx", "gy"),
            P(None, "gx", "gy"),
            P("shot", None),
            P("shot", None, None),
            P("shot"),
            P("shot"),
            P("shot", None),
            P("shot", None),
            P("shot", "gx", "gy"),
        ),
        out_specs=(P("shot", "gx", "gy"), P("shot", "gx", "gy"), P("shot", "gx", "gy")),
        check_vma=False,
    )
```

time: 500 us -> 49.1 us (0.10)
  the two profiles are of different devices: /device:TPU:7 before, /device:TPU:128 now
where the time goes in v1:
time: 49.1 us; the launch traced here: 48.7 us
  Pallas kernels  39.3 us (80%)
  local copies, waits for them, and re-layouts  5.2 us (11%)
  between operations  2.64 us (5%)
  other arithmetic  1.6 us (3%)
    pallas_call x1, Pallas kernels, local(): call(states, mats, wavelet, source_x, source_y, aperture.reshape(1), resi...  39.3 us
    unnamed x19, local copies, waits for them, and re-layouts  4.04 us
    squeeze x1, local copies, waits for them, and re-layouts, local(): adjoint_state[0]  1.16 us

profile of v1, /device:TPU:128, one launch (start us, length us, event | category | flops | bytes accessed | tf_op | source)
XLA Modules:
  0.0 48.7 jit_solution(9701962693034490980)
XLA Ops:
  0.6 1.2 %copy_bitcast_fusion = (bf16[9,16,8,128]{3,1,2,0:T(8,128)(2,1)S(1)}, bf16[9,16,8,128]{3,1,2,0:T(8,128)(2,1)S(1)}) fusion(bf16[1,9,16,8,128]{4,3,2,1,0:T(8,128)(2,1)} %param.13, bf16[1,9,16,8,128]{4,3,2,1,0:T(8,128)(2,1)} %param.12), kind=kLoop, calls=%fused_computation.1 | loop fusion | bytes 1179648 | tf_op jit(solution)/shard_map/squeeze | solution.py:329
  1.8 0.0 copy-start.1
  1.8 0.0 copy-start.2
  1.8 0.9 %maximum_bitcast_fusion.refs_0_ = bf16[18,8,16,128]{3,2,1,0:T(8,128)(2,1)} fusion(bf16[9,16,8,128]{3,1,2,0:T(8,128)(2,1)S(1)} %get-tuple-element.3, bf16[9,16,8,128]{3,1,2,0:T(8,128)(2,1)S(1)} %get-tuple-element.4), kind=kLoop, calls=%fused_computation | loop fusion | flops 294912 | bytes 1179648 | tf_op jit(solution)/shard_map/transpose | solution.py:329
  2.7 0.0 copy-done.1
  2.7 0.0 copy-done.2
  2.7 0.0 copy-start
  2.7 0.8 %copy-done = f32[16,8,128]{2,1,0:T(8,128)S(1)} copy-done((f32[16,8,128]{2,1,0:T(8,128)S(1)}, f32[16,8,128]{2,1,0:T(8,128)}, u32[]{:S(2)}) %copy-start) | copy-done | bytes 65560
  3.6 0.0 copy-start.6
  3.6 0.7 %maximum_bitcast_fusion.1.refs_1_ = f32[3,8,16,128]{3,2,1,0:T(8,128)} fusion(f32[1,16,8,128]{3,1,2,0:T(8,128)S(1)} %get-tuple-element.5, f32[1,16,8,128]{3,1,2,0:T(8,128)S(1)} %get-tuple-element.6, f32[1,16,8,128]{3,1,2,0:T(8,128)S(1)} %bitcast.20), kind=kLoop, calls=%fused_computation.3 | loop fusion | flops 98304 | bytes 393216 | tf_op jit(solution)/shard_map/transpose | solution.py:330
  4.3 0.0 copy-done.6
  4.3 0.6 %copy.32 = f32[1,3,256]{2,1,0:T(4,128)} copy(f32[1,3,256]{2,0,1:T(1,128)S(1)} %copy-done.6) | data formatting | bytes 6144
  6.8 39.3 %shard_map.139 = (f32[1,8,128]{2,1,0:T(8,128)}, f32[1,8,128]{2,1,0:T(8,128)}, f32[1,8,128]{2,1,0:T(8,128)}) custom-call(bf16[18,8,16,128]{3,2,1,0:T(8,128)(2,1)} %maximum_bitcast_fusion.refs_0_, f32[3,8,16,128]{3,2,1,0:T(8,128)} %maximum_bitcast_fusion.1.refs_1_, f32[1,3]{1,0:T(1,128)} %refs_2_.1, s32[1]{0:T(128)S(6)} %copy.36.refs_3_, s32[1]{0:T(128)S(6)} %copy.37.refs_4_, ...), custom_call_target="tpu_custom_call" | custom-call | tf_op jit(solution)/shard_map/pallas_call | solution.py:366
  46.1 0.0 copy-start.5
  46.1 0.7 %copy-done.5 = f32[1,8,128]{2,1,0:T(8,128)S(1)} copy-done((f32[1,8,128]{2,1,0:T(8,128)S(1)}, f32[1,8,128]{2,1,0:T(8,128)}, u32[]{:S(2)}) %copy-start.5) | copy-done | bytes 4120
  46.8 0.0 copy-start.4
  46.8 0.6 %copy.39 = f32[1,8,128]{2,1,0:T(8,128)} copy(f32[1,8,128]{2,1,0:T(8,128)S(1)} %copy-done.5) | data formatting | bytes 8192
  47.4 0.1 copy-done.4
  47.5 0.0 copy-start.3
  47.5 0.6 %copy.40 = f32[1,8,128]{2,1,0:T(8,128)} copy(f32[1,8,128]{2,1,0:T(8,128)S(1)} %copy-done.4) | data formatting | bytes 8192
  48.1 0.1 copy-done.3
  48.1 0.6 %copy.41 = f32[1,8,128]{2,1,0:T(8,128)} copy(f32[1,8,128]{2,1,0:T(8,128)S(1)} %copy-done.3) | data formatting | bytes 8192
  (2 shorter events, 0.0 us)
Async XLA Ops:
  1.8 0.9 %copy-start.1 = (f32[16,8,128]{2,1,0:T(8,128)S(1)}, f32[16,8,128]{2,1,0:T(8,128)}, u32[]{:S(2)}) copy-start(f32[16,8,128]{2,1,0:T(8,128)} %param.16) | copy-start | bytes 196612
  1.8 0.9 %copy-start.2 = (f32[16,8,128]{2,1,0:T(8,128)S(1)}, f32[16,8,128]{2,1,0:T(8,128)}, u32[]{:S(2)}) copy-start(f32[16,8,128]{2,1,0:T(8,128)} %param.15) | copy-start | bytes 196612
  2.7 0.8 %copy-start = (f32[16,8,128]{2,1,0:T(8,128)S(1)}, f32[16,8,128]{2,1,0:T(8,128)}, u32[]{:S(2)}) copy-start(f32[16,8,128]{2,1,0:T(8,128)} %param.14) | copy-start | bytes 196612
  3.6 0.7 %copy-start.6 = (f32[1,3,256]{2,0,1:T(1,128)S(1)}, f32[1,3,256]{2,0,1:T(1,128)}, u32[]{:S(2)}) copy-start(f32[1,3,256]{2,0,1:T(1,128)} %param.18) | copy-start | bytes 9220
  46.1 0.7 %copy-start.5 = (f32[1,8,128]{2,1,0:T(8,128)S(1)}, f32[1,8,128]{2,1,0:T(8,128)}, u32[]{:S(2)}) copy-start(f32[1,8,128]{2,1,0:T(8,128)} %get-tuple-element.10) | copy-start | bytes 12292
  46.8 0.7 %copy-start.4 = (f32[1,8,128]{2,1,0:T(8,128)S(1)}, f32[1,8,128]{2,1,0:T(8,128)}, u32[]{:S(2)}) copy-start(f32[1,8,128]{2,1,0:T(8,128)} %get-tuple-element.11) | copy-start | bytes 12292
  47.5 0.7 %copy-start.3 = (f32[1,8,128]{2,1,0:T(8,128)S(1)}, f32[1,8,128]{2,1,0:T(8,128)}, u32[]{:S(2)}) copy-start(f32[1,8,128]{2,1,0:T(8,128)} %get-tuple-element.12) | copy-start | bytes 12292

commit v2 on v1

--- a/solution.py
+++ b/solution.py
@@ -13,15 +13,32 @@
 
 def kernel(
     gx_tiles, gy_tiles, steps,
-    states, mats, wavelet, source_x, source_y, aperture, residual, receiver_x, receiver_y,
-    out_lambda, out_mu, out_rho,
-    field, model, x_low, x_high, m_low, m_high, pack, pack_low, pack_high,
+    forward_hbm, adjoint_hbm, lame_hbm, shear_hbm, density_hbm,
+    wavelet_hbm, residual_hbm, source_x_hbm, source_y_hbm, receiver_x_hbm, receiver_y_hbm, aperture_hbm,
+    out,
+    raw, raw_model, wavelet, residual, source_x, source_y, receiver_x, receiver_y, aperture, fetch,
+    edge_low, edge_high, edge_model, field, model, x_low, x_high, m_low, m_high, pack, pack_low, pack_high,
     strain, motion, lifted, term, chunks, got_core, sum_core, got_ring, sum_ring, got_half,
     send, recv,
 ):
-    fields2, cx, nz, cy = states.shape
-    runs = fields2 // 9
+    runs, fields, nz, cx, cy = raw.shape
+    fields2 = runs * fields
     wide = cx + 2 * HALO
+    sources = (
+        lame_hbm, shear_hbm, density_hbm, forward_hbm.at[0], adjoint_hbm.at[0], wavelet_hbm, residual_hbm,
+        source_x_hbm, source_y_hbm, receiver_x_hbm, receiver_y_hbm, aperture_hbm,
+    )
+    targets = (
+        raw_model.at[0], raw_model.at[1], raw_model.at[2], raw.at[0], raw.at[1], wavelet, residual,
+        source_x, source_y, receiver_x, receiver_y, aperture,
+    )
+    fetched = [
+        pltpu.make_async_copy(source, target, fetch.at[n])
+        for n, (source, target) in enumerate(zip(sources, targets))
+    ]
+    for copy in fetched:
+        copy.start()
+
     gx, gy, shot = lax.axis_index("gx"), lax.axis_index("gy"), lax.axis_index("shot")
     half, ring, core = shot // (RING * CORES), lax.rem(shot // CORES, RING), lax.rem(shot, CORES)
     x_start, y_start = gx * cx, gy * cy
@@ -54,25 +71,9 @@
         def _():
             pl.semaphore_signal(barrier, inc=1, device_id=tile(dx, dy), device_id_type=MESH)
 
-    lane = lax.broadcasted_iota(jnp.int32, (nz, cy), 1)
-
-    def pack_row(x, carry):
-        total = jnp.zeros((nz, cy), jnp.float32)
-        for f in range(fields2 + 3):
-            value = states[f, x].astype(jnp.float32) if f < fields2 else mats[f - fields2, x]
-            moved = pltpu.roll(value, 6 * f + 3, axis=1)
-            total = jnp.where((lane >= 6 * f) & (lane < 6 * f + 6), moved, total)
-        pack[x] = total
-        return carry
-
-    lax.fori_loop(0, cx, pack_row, 0)
-
     along_x = jnp.minimum(gx, 1) + jnp.minimum(gx_tiles - 1 - gx, 1) + 1
     along_y = jnp.minimum(gy, 1) + jnp.minimum(gy_tiles - 1 - gy, 1) + 1
     pl.semaphore_wait(barrier, along_x * along_y - 1 + len(peers))
-
-    def edge(dx):
-        return pl.ds(0, HALO) if dx < 0 else pl.ds(cx - HALO, HALO)
 
     messages = []
 
@@ -83,7 +84,7 @@
             device_id=tile(dx, dy), device_id_type=MESH)))
 
     for dx in (-1, 1):
-        message(dx, 0, mats.at[:, edge(dx)], m_high if dx < 0 else m_low)
+        message(dx, 0, edge_model.at[0 if dx < 0 else 1], m_high if dx < 0 else m_low)
     for dx in (-1, 0, 1):
         for dy in (-1, 1):
             side = pack_high if dy < 0 else pack_low
@@ -91,18 +92,59 @@
                 message(dx, dy, pack, side.at[pl.ds(HALO, cx)])
             else:
                 row = HALO + cx if dx < 0 else 0
-                message(dx, dy, pack.at[edge(dx)], side.at[pl.ds(row, HALO)])
+                source = pack.at[pl.ds(0 if dx < 0 else cx - HALO, HALO)]
+                message(dx, dy, source, side.at[pl.ds(row, HALO)])
     shared = len(messages)
     for run in range(runs):
         for dx in (-1, 1):
             side = x_high if dx < 0 else x_low
-            message(dx, 0, states.at[pl.ds(9 * run, 9), edge(dx)], side.at[run])
-    order = list(range(shared + 2)) + list(range(shared + 2, len(messages)))
-    for n in order:
-        dx, dy, copy = messages[n]
-        @pl.when(there(dx, dy))
-        def _():
-            copy.start()
+            message(dx, 0, (edge_low if dx < 0 else edge_high).at[run], side.at[run])
+
+    def issue(numbers):
+        for n in numbers:
+            dx, dy, copy = messages[n]
+            @pl.when(there(dx, dy))
+            def _():
+                copy.start()
+
+    for n in range(3):
+        fetched[n].wait()
+    for f in range(3):
+        value = raw_model[f]
+        if f == 2:
+            value = courant * (1.0 / value)
+        turned = jnp.swapaxes(value, 0, 1)
+        model[f, HALO : HALO + cx, :, 0:cy] = turned
+        edge_model[0, f] = turned[:HALO]
+        edge_model[1, f] = turned[cx - HALO :]
+    issue((0, 1))
+    for run in range(runs):
+        fetched[3 + run].wait()
+
+        def turn(f, carry):
+            turned = jnp.swapaxes(raw[run, f].astype(jnp.float32), 0, 1)
+            field[fields * run + f, HALO : HALO + cx, :, 0:cy] = turned
+            edge_low[run, f] = turned[:HALO].astype(jnp.bfloat16)
+            edge_high[run, f] = turned[cx - HALO :].astype(jnp.bfloat16)
+            return carry
+
+        lax.fori_loop(0, fields, turn, 0)
+        if run == 0:
+            issue((shared, shared + 1))
+
+    lane = lax.broadcasted_iota(jnp.int32, (nz, cy), 1)
+
+    def pack_row(x, carry):
+        total = jnp.zeros((nz, cy), jnp.float32)
+        for f in range(fields2 + 3):
+            value = (field[f, x + HALO] if f < fields2 else model[f - fields2, x + HALO])[:, 0:cy]
+            moved = pltpu.roll(value, 6 * f + 3, axis=1)
+            total = jnp.where((lane >= 6 * f) & (lane < 6 * f + 6), moved, total)
+        pack[x] = total
+        return carry
+
+    lax.fori_loop(0, cx, pack_row, 0)
+    issue(range(2, shared))
 
     def blank(dx, dy, ref):
         @pl.when(jnp.logical_not(there(dx, dy)))
@@ -117,14 +159,8 @@
             row, count = {-1: (0, HALO), 0: (HALO, cx), 1: (HALO + cx, HALO)}[dx]
             blank(dx, dy, side.at[pl.ds(row, count)])
 
-    def own_row(x, carry):
-        for f in range(fields2):
-            field[f, x + HALO, :, 0:cy] = states[f, x].astype(jnp.float32)
-        for f in range(3):
-            model[f, x + HALO, :, 0:cy] = mats[f, x]
-        return carry
-
-    lax.fori_loop(0, cx, own_row, 0)
+    for copy in fetched[5:]:
+        copy.wait()
 
     lanes2 = lax.broadcasted_iota(jnp.int32, (nz, 2 * cy), 1)
     depth = lax.broadcasted_iota(jnp.int32, (nz, 2 * cy), 0)
@@ -137,7 +173,7 @@
     cells = jnp.where(cells < cy + cy // 2, cells, cells - 2 * cy) + y_start
     hit_y = jnp.where(cells == receiver_y[...], 1.0, 0.0).astype(jnp.float32)
     for n in range(steps):
-        picked = jnp.where(hit_x, residual[n : n + 1, :], 0.0)
+        picked = jnp.where(hit_x, residual[n], 0.0)
         lifted[n] = lax.dot_general(
             picked, hit_y, (((1,), (1,)), ((), ())),
             precision=lax.Precision.HIGHEST, preferred_element_type=jnp.float32)
@@ -172,12 +208,13 @@
                 return carry
             lax.fori_loop(0, 9, body, 0)
 
-    for n in range(shared):
+    for n in range(shared + 2):
         wait_recv(n)
     for f in range(3):
         for x in range(HALO):
             model[f, x, :, 0:cy] = m_low[f, x]
             model[f, HALO + cx + x, :, 0:cy] = m_high[f, x]
+    issue(range(shared + 2, len(messages)))
     unpack_rows()
 
     first_z, last_z = depth == 0, depth == nz - 1
@@ -198,8 +235,9 @@
     lift_at = depth == 1
 
     for run in range(runs):
-        for n in (shared + 2 * run, shared + 2 * run + 1):
-            wait_recv(n)
+        if run == 1:
+            for n in (shared + 2, shared + 3):
+                wait_recv(n)
         x_halo(run)
         vx, vy, vz, sxx, syy, szz, sxy, sxz, syz = range(9 * run, 9 * run + 9)
         for n in range(steps):
@@ -254,7 +292,7 @@
 
             lax.fori_loop(n + 1, wide - 1 - n, stress, 0)
 
-    factor = (-courant / (HALVES * RING * CORES)) * aperture[0].astype(jnp.float32)
+    factor = (-courant / (HALVES * RING * CORES)) * aperture[0, 0, 0].astype(jnp.float32)
 
     def image(x, carry):
         k = x + HALO
@@ -307,7 +345,7 @@
     copy.wait_recv()
     last += rings + [copy]
     result = sum_ring[half] + got_half[...]
-    out_lambda[0], out_mu[0], out_rho[0] = result[0], result[1], result[2]
+    out[...] = result
     for copy in last:
         copy.wait_send()
     for dx, dy, copy in messages:
@@ -326,19 +364,31 @@
         nz, cx, cy = lame.shape
         steps = wavelet.shape[1]
         wide = cx + 2 * HALO
-        states = jnp.concatenate([forward_state[0], adjoint_state[0]]).swapaxes(1, 2)
-        mats = jnp.stack([lame, shear, courant * (1.0 / density)]).swapaxes(1, 2)
         f32 = jnp.float32
-        out = jax.ShapeDtypeStruct((1, cx, cy), f32)
+        out = jax.ShapeDtypeStruct((3, cx, cy), f32)
         vmem = pl.BlockSpec(memory_space=pltpu.VMEM)
-        smem = pl.BlockSpec(memory_space=pltpu.SMEM)
+        anywhere = pl.BlockSpec(memory_space=pl.ANY)
+        S = pltpu.SMEM
         V = pltpu.VMEM
         call = pl.pallas_call(
             lambda *refs: kernel(gx_tiles, gy_tiles, steps, *refs),
-            out_shape=(out, out, out),
-            in_specs=[vmem, vmem, smem, smem, smem, smem, vmem, vmem, vmem],
-            out_specs=(vmem, vmem, vmem),
+            out_shape=out,
+            in_specs=[anywhere] * 12,
+            out_specs=vmem,
             scratch_shapes=[
+                V((2, 9, nz, cx, cy), jnp.bfloat16),
+                V((3, nz, cx, cy), f32),
+                S((1, steps), f32),
+                V((steps, 1, residual.shape[2]), f32),
+                S((1,), jnp.int32),
+                S((1,), jnp.int32),
+                V((1, residual.shape[2]), jnp.int32),
+                V((1, residual.shape[2]), jnp.int32),
+                S((1, 1, 1), jnp.int32),
+                pltpu.SemaphoreType.DMA((12,)),
+                V((2, 9, HALO, nz, cy), jnp.bfloat16),
+                V((2, 9, HALO, nz, cy), jnp.bfloat16),
+                V((2, 3, HALO, nz, cy), f32),
                 V((18, wide, nz, 2 * cy), f32),
                 V((3, wide, nz, 2 * cy), f32),
                 V((2, 9, HALO, nz, cy), jnp.bfloat16),
@@ -363,10 +413,11 @@
             ],
             compiler_params=pltpu.CompilerParams(collective_id=0, has_side_effects=True),
         )
-        return call(
-            states, mats, wavelet, source_x, source_y, aperture.reshape(1),
-            residual[0], receiver_x, receiver_y,
+        sums = call(
+            forward_state, adjoint_state, lame, shear, density, wavelet, residual.swapaxes(0, 1),
+            source_x, source_y, receiver_x, receiver_y, aperture,
         )
+        return sums[0:1], sums[1:2], sums[2:3]
 
     return jax.shard_map(
         local,

time: 49.1 us -> 43.7 us (0.89)
  local copies, waits for them, and re-layouts: 5.2 us -> 1.29 us
  other arithmetic: 1.6 us -> 0 us
    unnamed x19 -> x0, local copies, waits for them, and re-layouts: 4.04 us -> none
    transpose x2 -> x0, other arithmetic: 1.56 us -> none  [the longest x1 0.87 us: local(): jnp.concatenate([forward_state[0], adjoint_state[0]]).swapaxes(1, 2)]
    slice x0 -> x1, local copies, waits for them, and re-layouts: none -> 1.29 us  [local(): return (sums[0:1], sums[1:2], sums[2:3])]
    squeeze x1 -> x0, local copies, waits for them, and re-layouts: 1.16 us -> none  [local(): adjoint_state[0]]
where the time goes in v2:
time: 43.7 us; the launch traced here: 43.5 us
  Pallas kernels  39.6 us (91%)
  between operations  2.58 us (6%)
  local copies, waits for them, and re-layouts  1.29 us (3%)
    pallas_call x1, Pallas kernels, local(): call(forward_state, adjoint_state, lame, shear, density, wavelet, residua...  39.6 us
    slice x1, local copies, waits for them, and re-layouts, local(): return (sums[0:1], sums[1:2], sums[2:3])  1.29 us

profile of v2, /device:TPU:128, one launch (start us, length us, event | category | flops | bytes accessed | tf_op | source)
XLA Modules:
  0.0 43.5 jit_solution(13384748097662762879)
XLA Ops:
  2.6 39.6 %shard_map.139 = f32[3,8,128]{2,1,0:T(8,128)} custom-call(bf16[1,9,16,8,128]{4,3,2,1,0:T(8,128)(2,1)} %refs_0_.1, bf16[1,9,16,8,128]{4,3,2,1,0:T(8,128)(2,1)} %refs_1_.1, f32[16,8,128]{2,1,0:T(8,128)} %refs_2_.1, f32[16,8,128]{2,1,0:T(8,128)} %refs_3_.1, f32[16,8,128]{2,1,0:T(8,128)} %refs_4_.1, f32[1,3]{1,0:T(1,128)} %refs_5_.1, f32[3,1,256]{2,1,0:T(1,128)} %bitcast.1, ...), custom_call_target="tpu_custom_call" | custom-call | tf_op jit(solution)/shard_map/pallas_call | solution.py:416
  42.2 1.3 %fusion = (f32[1,8,128]{2,1,0:T(8,128)}, f32[1,8,128]{2,1,0:T(8,128)}, f32[1,8,128]{2,1,0:T(8,128)}) fusion(f32[3,8,128]{2,1,0:T(8,128)} %shard_map.139), kind=kLoop, calls=%fused_computation | loop fusion | bytes 24576 | tf_op jit(solution)/shard_map/slice | solution.py:420

commit v3 on v2

--- a/solution.py
+++ b/solution.py
@@ -144,7 +144,7 @@
         return carry
 
     lax.fori_loop(0, cx, pack_row, 0)
-    issue(range(2, shared))
+    issue((4, 5, 2, 3, 6, 7, shared + 2, shared + 3))
 
     def blank(dx, dy, ref):
         @pl.when(jnp.logical_not(there(dx, dy)))
@@ -187,110 +187,116 @@
     lane6 = lax.rem(lane, 6)
     at_edge = (lane < HALO) | (lane >= cy - HALO)
 
-    def unpack_rows():
-        def body(x, carry):
-            both = jnp.where(lane6 < 3, pack_low[x], pack_high[x])
-            for f in range(fields2 + 3):
-                moved = pltpu.roll(both, (cy - HALO - 6 * f) % cy, axis=1)
-                moved = jnp.where(at_edge, moved, 0.0)
-                if f < fields2:
-                    field[f, x, :, cy : 2 * cy] = moved
-                else:
-                    model[f - fields2, x, :, cy : 2 * cy] = moved
+    def unpack_row(x):
+        both = jnp.where(lane6 < 3, pack_low[x], pack_high[x])
+        for f in range(fields2 + 3):
+            moved = pltpu.roll(both, (cy - HALO - 6 * f) % cy, axis=1)
+            moved = jnp.where(at_edge, moved, 0.0)
+            if f < fields2:
+                field[f, x, :, cy : 2 * cy] = moved
+            else:
+                model[f - fields2, x, :, cy : 2 * cy] = moved
+
+    def loop(low, high, *bodies):
+        def body(i, carry):
+            for one in bodies:
+                one(i)
             return carry
-        lax.fori_loop(0, wide, body, 0)
+        lax.fori_loop(low, high, body, 0)
 
     def x_halo(run):
-        for x in range(HALO):
-            def body(f, carry):
+        def body(f):
+            for x in range(HALO):
                 field[9 * run + f, x, :, 0:cy] = x_low[run, f, x].astype(jnp.float32)
                 field[9 * run + f, HALO + cx + x, :, 0:cy] = x_high[run, f, x].astype(jnp.float32)
-                return carry
-            lax.fori_loop(0, 9, body, 0)
-
-    for n in range(shared + 2):
+        loop(0, 9, body)
+
+    first_z, last_z = depth == 0, depth == nz - 1
+
+    def y_next(v):
+        return pltpu.roll(v, 2 * cy - 1, axis=1)
+
+    def y_back(v):
+        return pltpu.roll(v, 1, axis=1)
+
+    def z_next(v):
+        return jnp.where(last_z, 0.0, pltpu.roll(v, nz - 1, axis=0))
+
+    def z_back(v):
+        return jnp.where(first_z, 0.0, pltpu.roll(v, 1, axis=0))
+
+    pulse_at = jnp.where((depth == 2) & (column == source_y[0]), 1.0, 0.0).astype(jnp.float32)
+    lift_at = depth == 1
+
+    def velocity(run, n, j):
+        vx, vy, vz, sxx, syy, szz, sxy, sxz, syz = range(9 * run, 9 * run + 9)
+        k = j + 1
+        b0, b1 = model[2, j], model[2, k]
+        xy0, xy1, xz0, xz1 = field[sxy, j], field[sxy, k], field[sxz, j], field[sxz, k]
+        yy, zz, yz = field[syy, k], field[szz, k], field[syz, k]
+        gain_x = b0 * ((field[sxx, k] - field[sxx, j]) + (xy0 - y_back(xy0)) + (xz0 - z_back(xz0)))
+        gain_y = b1 * ((xy1 - xy0) + (y_next(yy) - yy) + (yz - z_back(yz)))
+        gain_z = b1 * ((xz1 - xz0) + (yz - y_back(yz)) + (z_next(zz) - zz))
+        new_x, new_y = field[vx, j] + gain_x, field[vy, k] + gain_y
+        new_z = field[vz, k] + gain_z
+        if run == 1:
+            row = lifted[steps - 1 - n, pl.ds(k, 1), :]
+            new_z = new_z + jnp.where(lift_at, row, 0.0)
+        field[vx, j], field[vy, k], field[vz, k] = new_x, new_y, new_z
+        if run == 0:
+            saved = (gain_x * (1.0 / courant), gain_y * (1.0 / courant), gain_z * (1.0 / courant))
+        else:
+            saved = (new_x, new_y, new_z)
+        motion[run, n, 0, j] = saved[0][:, 0:cy]
+        motion[run, n, 1, k] = saved[1][:, 0:cy]
+        motion[run, n, 2, k] = saved[2][:, 0:cy]
+
+    def stress(run, n, k):
+        vx, vy, vz, sxx, syy, szz, sxy, sxz, syz = range(9 * run, 9 * run + 9)
+        x0, y0, z0 = field[vx, k], field[vy, k], field[vz, k]
+        e = (
+            x0 - field[vx, k - 1],
+            y0 - y_back(y0),
+            z0 - z_back(z0),
+            (y_next(x0) - x0) + (field[vy, k + 1] - y0),
+            (z_next(x0) - x0) + (field[vz, k + 1] - z0),
+            (z_next(y0) - y0) + (y_next(z0) - z0),
+        )
+        for c in range(6):
+            strain[run, n, c, k] = e[c][:, 0:cy]
+        if n < steps - 1:
+            scaled = courant * model[1, k]
+            bulk = courant * model[0, k] * (e[0] + e[1] + e[2])
+            if run == 0:
+                amount = jnp.where(x_start + k - HALO == source_x[0], wavelet[0, n], 0.0)
+                bulk = bulk + amount * pulse_at
+            for c in range(3):
+                field[sxx + c, k] = field[sxx + c, k] + (bulk + 2.0 * scaled * e[c])
+            for c in range(3, 6):
+                field[sxx + c, k] = field[sxx + c, k] + scaled * e[c]
+
+    wait_recv(4)
+    wait_recv(5)
+    loop(0, cx, lambda x: unpack_row(x + HALO))
+    for n in range(steps):
+        loop(HALO + n, cx + HALO - 1 - n, lambda j: velocity(0, n, j), lambda j: velocity(1, n, j))
+        loop(HALO + 1 + n, cx + HALO - 1 - n, lambda k: stress(0, n, k), lambda k: stress(1, n, k))
+
+    for n in (0, 1, 2, 3, 6, 7):
         wait_recv(n)
     for f in range(3):
         for x in range(HALO):
             model[f, x, :, 0:cy] = m_low[f, x]
             model[f, HALO + cx + x, :, 0:cy] = m_high[f, x]
-    issue(range(shared + 2, len(messages)))
-    unpack_rows()
-
-    first_z, last_z = depth == 0, depth == nz - 1
-
-    def y_next(v):
-        return pltpu.roll(v, 2 * cy - 1, axis=1)
-
-    def y_back(v):
-        return pltpu.roll(v, 1, axis=1)
-
-    def z_next(v):
-        return jnp.where(last_z, 0.0, pltpu.roll(v, nz - 1, axis=0))
-
-    def z_back(v):
-        return jnp.where(first_z, 0.0, pltpu.roll(v, 1, axis=0))
-
-    pulse_at = jnp.where((depth == 2) & (column == source_y[0]), 1.0, 0.0).astype(jnp.float32)
-    lift_at = depth == 1
-
+    loop(0, HALO, unpack_row, lambda x: unpack_row(x + HALO + cx))
     for run in range(runs):
-        if run == 1:
-            for n in (shared + 2, shared + 3):
-                wait_recv(n)
+        wait_recv(shared + 2 * run)
+        wait_recv(shared + 2 * run + 1)
         x_halo(run)
-        vx, vy, vz, sxx, syy, szz, sxy, sxz, syz = range(9 * run, 9 * run + 9)
         for n in range(steps):
-            def velocity(j, carry):
-                k = j + 1
-                b0, b1 = model[2, j], model[2, k]
-                xy0, xy1, xz0, xz1 = field[sxy, j], field[sxy, k], field[sxz, j], field[sxz, k]
-                yy, zz, yz = field[syy, k], field[szz, k], field[syz, k]
-                gain_x = b0 * ((field[sxx, k] - field[sxx, j]) + (xy0 - y_back(xy0)) + (xz0 - z_back(xz0)))
-                gain_y = b1 * ((xy1 - xy0) + (y_next(yy) - yy) + (yz - z_back(yz)))
-                gain_z = b1 * ((xz1 - xz0) + (yz - y_back(yz)) + (z_next(zz) - zz))
-                new_x, new_y = field[vx, j] + gain_x, field[vy, k] + gain_y
-                new_z = field[vz, k] + gain_z
-                if run == 1:
-                    row = lifted[steps - 1 - n, pl.ds(k, 1), :]
-                    new_z = new_z + jnp.where(lift_at, row, 0.0)
-                field[vx, j], field[vy, k], field[vz, k] = new_x, new_y, new_z
-                if run == 0:
-                    saved = (gain_x * (1.0 / courant), gain_y * (1.0 / courant), gain_z * (1.0 / courant))
-                else:
-                    saved = (new_x, new_y, new_z)
-                motion[run, n, 0, j] = saved[0][:, 0:cy]
-                motion[run, n, 1, k] = saved[1][:, 0:cy]
-                motion[run, n, 2, k] = saved[2][:, 0:cy]
-                return carry
-
-            lax.fori_loop(n, wide - 1 - n, velocity, 0)
-
-            def stress(k, carry):
-                x0, y0, z0 = field[vx, k], field[vy, k], field[vz, k]
-                e = (
-                    x0 - field[vx, k - 1],
-                    y0 - y_back(y0),
-                    z0 - z_back(z0),
-                    (y_next(x0) - x0) + (field[vy, k + 1] - y0),
-                    (z_next(x0) - x0) + (field[vz, k + 1] - z0),
-                    (z_next(y0) - y0) + (y_next(z0) - z0),
-                )
-                for c in range(6):
-                    strain[run, n, c, k] = e[c][:, 0:cy]
-                if n < steps - 1:
-                    scaled = courant * model[1, k]
-                    bulk = courant * model[0, k] * (e[0] + e[1] + e[2])
-                    if run == 0:
-                        amount = jnp.where(x_start + k - HALO == source_x[0], wavelet[0, n], 0.0)
-                        bulk = bulk + amount * pulse_at
-                    for c in range(3):
-                        field[sxx + c, k] = field[sxx + c, k] + (bulk + 2.0 * scaled * e[c])
-                    for c in range(3, 6):
-                        field[sxx + c, k] = field[sxx + c, k] + scaled * e[c]
-                return carry
-
-            lax.fori_loop(n + 1, wide - 1 - n, stress, 0)
+            high = cx + HALO - 1 - n
+            loop(0, HALO, lambda i: velocity(run, n, i + n), lambda i: velocity(run, n, i + high))
+            loop(0, HALO, lambda i: stress(run, n, i + n + 1), lambda i: stress(run, n, i + high))
 
     factor = (-courant / (HALVES * RING * CORES)) * aperture[0, 0, 0].astype(jnp.float32)
 

time: 43.7 us -> 36.9 us (0.84)
  the two profiles are of different devices: /device:TPU:128 before, /device:TPU:136 now
where the time goes in v3:
time: 36.9 us; the launch traced here: 36.7 us
  Pallas kernels  32.8 us (89%)
  between operations  2.58 us (7%)
  local copies, waits for them, and re-layouts  1.29 us (3%)
    pallas_call x1, Pallas kernels, local(): call(forward_state, adjoint_state, lame, shear, density, wavelet, residua...  32.8 us
    slice x1, local copies, waits for them, and re-layouts, local(): return (sums[0:1], sums[1:2], sums[2:3])  1.29 us

profile of v3, /device:TPU:136, one launch (start us, length us, event | category | flops | bytes accessed | tf_op | source)
XLA Modules:
  0.0 36.7 jit_solution(12091952420014643079)
XLA Ops:
  2.6 32.8 %shard_map.139 = f32[3,8,128]{2,1,0:T(8,128)} custom-call(bf16[1,9,16,8,128]{4,3,2,1,0:T(8,128)(2,1)} %refs_0_.1, bf16[1,9,16,8,128]{4,3,2,1,0:T(8,128)(2,1)} %refs_1_.1, f32[16,8,128]{2,1,0:T(8,128)} %refs_2_.1, f32[16,8,128]{2,1,0:T(8,128)} %refs_3_.1, f32[16,8,128]{2,1,0:T(8,128)} %refs_4_.1, f32[1,3]{1,0:T(1,128)} %refs_5_.1, f32[3,1,256]{2,1,0:T(1,128)} %bitcast.1, ...), custom_call_target="tpu_custom_call" | custom-call | tf_op jit(solution)/shard_map/pallas_call | solution.py:422
  35.4 1.3 %fusion = (f32[1,8,128]{2,1,0:T(8,128)}, f32[1,8,128]{2,1,0:T(8,128)}, f32[1,8,128]{2,1,0:T(8,128)}) fusion(f32[3,8,128]{2,1,0:T(8,128)} %shard_map.139), kind=kLoop, calls=%fused_computation | loop fusion | bytes 24576 | tf_op jit(solution)/shard_map/slice | solution.py:426

commit v4 on v3

--- a/solution.py
+++ b/solution.py
@@ -71,10 +71,6 @@
         def _():
             pl.semaphore_signal(barrier, inc=1, device_id=tile(dx, dy), device_id_type=MESH)
 
-    along_x = jnp.minimum(gx, 1) + jnp.minimum(gx_tiles - 1 - gx, 1) + 1
-    along_y = jnp.minimum(gy, 1) + jnp.minimum(gy_tiles - 1 - gy, 1) + 1
-    pl.semaphore_wait(barrier, along_x * along_y - 1 + len(peers))
-
     messages = []
 
     def message(dx, dy, source, target):
@@ -117,7 +113,6 @@
         model[f, HALO : HALO + cx, :, 0:cy] = turned
         edge_model[0, f] = turned[:HALO]
         edge_model[1, f] = turned[cx - HALO :]
-    issue((0, 1))
     for run in range(runs):
         fetched[3 + run].wait()
 
@@ -130,20 +125,29 @@
 
         lax.fori_loop(0, fields, turn, 0)
         if run == 0:
-            issue((shared, shared + 1))
+            along_x = jnp.minimum(gx, 1) + jnp.minimum(gx_tiles - 1 - gx, 1) + 1
+            along_y = jnp.minimum(gy, 1) + jnp.minimum(gy_tiles - 1 - gy, 1) + 1
+            pl.semaphore_wait(barrier, along_x * along_y - 1 + len(peers))
+            issue((0, 1, shared, shared + 1))
+
+    def loop(low, high, *bodies):
+        def body(i, carry):
+            for one in bodies:
+                one(i)
+            return carry
+        lax.fori_loop(low, high, body, 0)
 
     lane = lax.broadcasted_iota(jnp.int32, (nz, cy), 1)
 
-    def pack_row(x, carry):
+    def pack_row(x):
         total = jnp.zeros((nz, cy), jnp.float32)
         for f in range(fields2 + 3):
             value = (field[f, x + HALO] if f < fields2 else model[f - fields2, x + HALO])[:, 0:cy]
             moved = pltpu.roll(value, 6 * f + 3, axis=1)
             total = jnp.where((lane >= 6 * f) & (lane < 6 * f + 6), moved, total)
         pack[x] = total
-        return carry
-
-    lax.fori_loop(0, cx, pack_row, 0)
+
+    loop(0, cx // 2, pack_row, lambda x: pack_row(x + cx // 2))
     issue((4, 5, 2, 3, 6, 7, shared + 2, shared + 3))
 
     def blank(dx, dy, ref):
@@ -196,13 +200,6 @@
                 field[f, x, :, cy : 2 * cy] = moved
             else:
                 model[f - fields2, x, :, cy : 2 * cy] = moved
-
-    def loop(low, high, *bodies):
-        def body(i, carry):
-            for one in bodies:
-                one(i)
-            return carry
-        lax.fori_loop(low, high, body, 0)
 
     def x_halo(run):
         def body(f):
@@ -277,7 +274,7 @@
 
     wait_recv(4)
     wait_recv(5)
-    loop(0, cx, lambda x: unpack_row(x + HALO))
+    loop(0, cx // 2, lambda x: unpack_row(x + HALO), lambda x: unpack_row(x + HALO + cx // 2))
     for n in range(steps):
         loop(HALO + n, cx + HALO - 1 - n, lambda j: velocity(0, n, j), lambda j: velocity(1, n, j))
         loop(HALO + 1 + n, cx + HALO - 1 - n, lambda k: stress(0, n, k), lambda k: stress(1, n, k))
@@ -300,7 +297,7 @@
 
     factor = (-courant / (HALVES * RING * CORES)) * aperture[0, 0, 0].astype(jnp.float32)
 
-    def image(x, carry):
+    def image(x):
         k = x + HALO
         first = second = third = jnp.zeros((nz, cy), jnp.float32)
         for m in range(steps):
@@ -313,45 +310,46 @@
             for c in range(3):
                 third = third + motion[0, n, c, k] * motion[1, m, c, k]
         term[0, x], term[1, x], term[2, x] = factor * first, factor * second, factor * third
-        return carry
-
-    lax.fori_loop(0, cx, image, 0)
+
+    loop(0, cx // 2, image, lambda x: image(x + cx // 2))
 
     for t in range(3):
         turned = jnp.swapaxes(term[t], 0, 1)
         for z in range(nz):
             chunks[z % CORES, z // (CORES * RING), (z // CORES) % RING, t] = turned[z]
 
-    base = len(messages)
-    copy = pltpu.make_async_remote_copy(
-        src_ref=chunks.at[1 - core], dst_ref=got_core, send_sem=send.at[base], recv_sem=recv.at[base],
-        device_id=peers[0], device_id_type=MESH)
-    copy.start()
-    copy.wait_recv()
-    last = [copy]
-    sum_core[...] = chunks[core] + got_core[...]
+    count = len(messages)
+    last = []
+
+    def push(source, target, peer):
+        n = count + len(last)
+        copy = pltpu.make_async_remote_copy(
+            src_ref=source, dst_ref=target, send_sem=send.at[n], recv_sem=recv.at[n],
+            device_id=peer, device_id_type=MESH)
+        copy.start()
+        last.append(copy)
+        return copy
+
+    groups = (1 - half, half)
+    cores = [push(chunks.at[1 - core, g], got_core.at[n], peers[0]) for n, g in enumerate(groups)]
     rings = []
-    for d in range(1, RING):
-        copy = pltpu.make_async_remote_copy(
-            src_ref=sum_core.at[:, lax.rem(ring + d, RING)], dst_ref=got_ring.at[d - 1],
-            send_sem=send.at[base + d], recv_sem=recv.at[base + d],
-            device_id=peers[d], device_id_type=MESH)
-        copy.start()
-        rings.append(copy)
-    total = sum_core[:, ring]
-    for d in range(1, RING):
-        rings[d - 1].wait_recv()
-        total = total + got_ring[d - 1]
-    sum_ring[...] = total
-    copy = pltpu.make_async_remote_copy(
-        src_ref=sum_ring.at[1 - half], dst_ref=got_half,
-        send_sem=send.at[base + RING], recv_sem=recv.at[base + RING],
-        device_id=peers[RING], device_id_type=MESH)
-    copy.start()
-    copy.wait_recv()
-    last += rings + [copy]
-    result = sum_ring[half] + got_half[...]
-    out[...] = result
+    for n, g in enumerate(groups):
+        cores[n].wait_recv()
+        sum_core[n] = chunks[core, g] + got_core[n]
+        rings.append([
+            push(sum_core.at[n, lax.rem(ring + d, RING)], got_ring.at[n, d - 1], peers[d])
+            for d in range(1, RING)
+        ])
+    for n in range(HALVES):
+        total = sum_core[n, ring]
+        for d in range(1, RING):
+            rings[n][d - 1].wait_recv()
+            total = total + got_ring[n, d - 1]
+        if n == 0:
+            sum_ring[...] = total
+            across = push(sum_ring, got_half, peers[RING])
+    across.wait_recv()
+    out[...] = total + got_half[...]
     for copy in last:
         copy.wait_send()
     for dx, dy, copy in messages:
@@ -411,11 +409,11 @@
                 V((CORES, HALVES, RING, 3, cx, cy), f32),
                 V((HALVES, RING, 3, cx, cy), f32),
                 V((HALVES, RING, 3, cx, cy), f32),
-                V((RING - 1, HALVES, 3, cx, cy), f32),
-                V((HALVES, 3, cx, cy), f32),
+                V((HALVES, RING - 1, 3, cx, cy), f32),
                 V((3, cx, cy), f32),
-                pltpu.SemaphoreType.DMA((17,)),
-                pltpu.SemaphoreType.DMA((17,)),
+                V((3, cx, cy), f32),
+                pltpu.SemaphoreType.DMA((21,)),
+                pltpu.SemaphoreType.DMA((21,)),
             ],
             compiler_params=pltpu.CompilerParams(collective_id=0, has_side_effects=True),
         )

time: 36.9 us -> 35.8 us (0.970)
  the two profiles are of different devices: /device:TPU:136 before, /device:TPU:128 now
where the time goes in v4:
time: 35.8 us; the launch traced here: 35.6 us
  Pallas kernels  31.8 us (89%)
  between operations  2.58 us (7%)
  local copies, waits for them, and re-layouts  1.29 us (4%)
    pallas_call x1, Pallas kernels, local(): call(forward_state, adjoint_state, lame, shear, density, wavelet, residua...  31.8 us
    slice x1, local copies, waits for them, and re-layouts, local(): return (sums[0:1], sums[1:2], sums[2:3])  1.29 us

profile of v4, /device:TPU:128, one launch (start us, length us, event | category | flops | bytes accessed | tf_op | source)
XLA Modules:
  0.0 35.6 jit_solution(10954823359705401505)
XLA Ops:
  2.6 31.8 %shard_map.139 = f32[3,8,128]{2,1,0:T(8,128)} custom-call(bf16[1,9,16,8,128]{4,3,2,1,0:T(8,128)(2,1)} %refs_0_.1, bf16[1,9,16,8,128]{4,3,2,1,0:T(8,128)(2,1)} %refs_1_.1, f32[16,8,128]{2,1,0:T(8,128)} %refs_2_.1, f32[16,8,128]{2,1,0:T(8,128)} %refs_3_.1, f32[16,8,128]{2,1,0:T(8,128)} %refs_4_.1, f32[1,3]{1,0:T(1,128)} %refs_5_.1, f32[3,1,256]{2,1,0:T(1,128)} %bitcast.1, ...), custom_call_target="tpu_custom_call" | custom-call | tf_op jit(solution)/shard_map/pallas_call | solution.py:420
  34.3 1.3 %fusion = (f32[1,8,128]{2,1,0:T(8,128)}, f32[1,8,128]{2,1,0:T(8,128)}, f32[1,8,128]{2,1,0:T(8,128)}) fusion(f32[3,8,128]{2,1,0:T(8,128)} %shard_map.139), kind=kLoop, calls=%fused_computation | loop fusion | bytes 24576 | tf_op jit(solution)/shard_map/slice | solution.py:424

commit v5 on v4

--- a/solution.py
+++ b/solution.py
@@ -290,10 +290,14 @@
         wait_recv(shared + 2 * run)
         wait_recv(shared + 2 * run + 1)
         x_halo(run)
-        for n in range(steps):
-            high = cx + HALO - 1 - n
-            loop(0, HALO, lambda i: velocity(run, n, i + n), lambda i: velocity(run, n, i + high))
-            loop(0, HALO, lambda i: stress(run, n, i + n + 1), lambda i: stress(run, n, i + high))
+    for n in range(steps):
+        high = cx + HALO - 1 - n
+        loop(0, HALO, *[
+            lambda i, run=run, row=row: velocity(run, n, i + row) for run in range(runs) for row in (n, high)
+        ])
+        loop(0, HALO, *[
+            lambda i, run=run, row=row: stress(run, n, i + row) for run in range(runs) for row in (n + 1, high)
+        ])
 
     factor = (-courant / (HALVES * RING * CORES)) * aperture[0, 0, 0].astype(jnp.float32)
 

time: 35.8 us -> 34.6 us (0.966)
  Pallas kernels: 31.8 us -> 30.5 us
    pallas_call x1, Pallas kernels: 31.8 us -> 30.5 us  [local(): call(forward_state, adjoint_state, lame, shear, density, wavelet, residua...]
where the time goes in v5:
time: 34.6 us; the launch traced here: 34.4 us
  Pallas kernels  30.5 us (88%)
  between operations  2.58 us (7%)
  local copies, waits for them, and re-layouts  1.29 us (4%)
    pallas_call x1, Pallas kernels, local(): call(forward_state, adjoint_state, lame, shear, density, wavelet, residua...  30.5 us
    slice x1, local copies, waits for them, and re-layouts, local(): return (sums[0:1], sums[1:2], sums[2:3])  1.29 us

profile of v5, /device:TPU:128, one launch (start us, length us, event | category | flops | bytes accessed | tf_op | source)
XLA Modules:
  0.0 34.4 jit_solution(14302820328749816815)
XLA Ops:
  2.6 30.5 %shard_map.139 = f32[3,8,128]{2,1,0:T(8,128)} custom-call(bf16[1,9,16,8,128]{4,3,2,1,0:T(8,128)(2,1)} %refs_0_.1, bf16[1,9,16,8,128]{4,3,2,1,0:T(8,128)(2,1)} %refs_1_.1, f32[16,8,128]{2,1,0:T(8,128)} %refs_2_.1, f32[16,8,128]{2,1,0:T(8,128)} %refs_3_.1, f32[16,8,128]{2,1,0:T(8,128)} %refs_4_.1, f32[1,3]{1,0:T(1,128)} %refs_5_.1, f32[3,1,256]{2,1,0:T(1,128)} %bitcast.1, ...), custom_call_target="tpu_custom_call" | custom-call | tf_op jit(solution)/shard_map/pallas_call | solution.py:424
  33.1 1.3 %fusion = (f32[1,8,128]{2,1,0:T(8,128)}, f32[1,8,128]{2,1,0:T(8,128)}, f32[1,8,128]{2,1,0:T(8,128)}) fusion(f32[3,8,128]{2,1,0:T(8,128)} %shard_map.139), kind=kLoop, calls=%fused_computation | loop fusion | bytes 24576 | tf_op jit(solution)/shard_map/slice | solution.py:428
